TPU v7x, 32 devices: a whole 2x2x4 slice. The times are simulated.
32 devices in a mesh: ctx: 8 (over z, y), tp: 4 (over x, core).
Axes of the slice: x: 2, y: 2, z: 4, core: 2. Of those that a mesh axis runs over, the one named last changes fastest.
Arguments:
- grad_out: bfloat16 [1024, 8192], P('ctx', 'tp'), may hold values from -40 to 40
- query_in: bfloat16 [1024, 8192], P('ctx', 'tp'), may hold values from -6 to 6
- key_in: bfloat16 [1024, 8192], P('ctx', 'tp'), may hold values from -6 to 6
- value_in: bfloat16 [1024, 8192], P('ctx', 'tp'), may hold values from -6 to 6
- residue: float32 [8192, 16], P('tp'), may hold values from -4 to 4
- log_rate: float32 [8192, 16], P('tp'), may hold values from -14 to -3, as said below
Outputs:
- grad_query: bfloat16 [1024, 8192], P('ctx', 'tp')
- grad_key: bfloat16 [1024, 8192], P('ctx', 'tp')
- grad_value: bfloat16 [1024, 8192], P('ctx', 'tp')
- residue_grad: float32 [8192, 16], P('tp')
- rate_grad: float32 [8192, 16], P('tp')
Inputs may be any that keep to these rules, and one draw needn't show every extreme that they name: `log_rate`: exp of an entry is the decay per position of one filter mode.
All inputs are finite; a program needn't handle non-finite values.
Results may differ from a plain program's by a relative error of at most 0.001.
Values sent between devices are 32-bit elements; how exact they have to be, the bound alone decides.
A program may use at most 64 MiB of HBM per device.

v0:
```python
import jax
import jax.numpy as jnp
from jax import lax
from jax.sharding import PartitionSpec as P

CLIP_NORM = 512


highest = lax.Precision.HIGHEST


def entering(part, axis, combine, identity, reverse):
    count = lax.axis_size(axis)
    place = lax.axis_index(axis)
    ahead = count - 1 - place if reverse else place
    gathered = jax.tree.map(lambda a: lax.all_gather(a, axis), part)
    state = jax.tree.map(lambda a, e: jnp.zeros_like(a) + jnp.asarray(e, a.dtype), part, identity)

    def one(turn, state):
        source = count - 1 - turn if reverse else turn
        return combine(
            state, jax.tree.map(lambda a: lax.dynamic_index_in_dim(a, source, 0, False), gathered)
        )

    return lax.fori_loop(0, ahead, one, state)


def paired(earlier, latter):
    return (earlier[0] * latter[0], latter[0] * earlier[1] + latter[1])


def per_device(grad_out, query_in, key_in, value_in, residue, log_rate):
    tok_rows, chan_count = grad_out.shape
    block_len = 16
    blocks = tok_rows // block_len
    rate_t = jnp.exp(log_rate).T
    step_t = jnp.exp(-rate_t)
    weight_t = residue.T * jnp.sqrt(2.0 * rate_t)
    offsets = jnp.arange(block_len, dtype=jnp.float32)
    powers = jnp.exp(-rate_t[:, None, :] * offsets[None, :, None])
    rev_powers = powers[:, ::-1, :]
    block_decay = jnp.exp(-rate_t * block_len)
    product = (key_in.astype(jnp.float32) * value_in.astype(jnp.float32)).reshape(
        blocks, block_len, chan_count
    )
    gated_grad = (grad_out.astype(jnp.float32) * query_in.astype(jnp.float32)).reshape(
        blocks, block_len, chan_count
    )
    target_pos = jnp.arange(block_len)[:, None]
    source_pos = jnp.arange(block_len)[None, :]
    lag_table = (
        (target_pos - source_pos)[None, :, :] == jnp.arange(block_len)[:, None, None]
    ).astype(jnp.float32)
    lag_table = lag_table.reshape(block_len, block_len * block_len)
    kernel_lags = jnp.sum(powers * weight_t[:, None, :], axis=0)
    toeplitz = jnp.dot(lag_table.T, kernel_lags, precision=highest).reshape(
        block_len, block_len, chan_count
    )
    end_states = jnp.sum(product[:, None, :, :] * rev_powers[None, :, :, :], axis=2)
    start_adj = jnp.sum(gated_grad[:, None, :, :] * powers[None, :, :, :], axis=2)
    block_power = jnp.broadcast_to(block_decay[None, :, :], end_states.shape)
    _, inc_states = lax.associative_scan(paired, (block_power, end_states), axis=0)
    _, inc_adj = lax.associative_scan(paired, (block_power, start_adj), axis=0, reverse=True)
    dev_state = inc_states[-1]
    dev_adj = inc_adj[0]
    zero_state = jnp.zeros_like(rate_t)

    def counted(earlier, latter):
        span_decay = jnp.exp(-rate_t * (tok_rows * latter[0]))
        return (earlier[0] + latter[0], span_decay * earlier[1] + latter[1])

    unit_count = jnp.ones((), jnp.float32)
    empty_count = jnp.zeros((), jnp.float32)
    _, carry_in = entering(
        (unit_count, dev_state), "ctx", counted, (empty_count, zero_state), False
    )
    _, carry_back = entering((unit_count, dev_adj), "ctx", counted, (empty_count, zero_state), True)
    conv_local = jnp.sum(toeplitz[None, :, :, :] * product[:, None, :, :], axis=2)
    back_local = jnp.sum(toeplitz[None, :, :, :] * gated_grad[:, :, None, :], axis=1)
    correlation = jnp.sum(gated_grad[:, :, None, :] * product[:, None, :, :], axis=0).reshape(
        block_len * block_len, chan_count
    )
    lag_sums = jnp.dot(lag_table, correlation, precision=highest)
    intra_weight = jnp.sum(lag_sums[None, :, :] * powers, axis=1)
    intra_lag = jnp.sum((lag_sums * offsets[:, None])[None, :, :] * powers, axis=1)
    in_weights = rev_powers * (block_len - offsets)[None, :, None]
    out_weights = powers * offsets[None, :, None]
    weighted_in = jnp.sum(product[:, None, :, :] * in_weights[None, :, :, :], axis=2)
    weighted_out = jnp.sum(gated_grad[:, None, :, :] * out_weights[None, :, :, :], axis=2)
    block_index = jnp.arange(blocks, dtype=jnp.float32)
    rise_power = jnp.exp(-rate_t[None, :, :] * (block_len * block_index)[:, None, None])
    fall_power = jnp.exp(
        -rate_t[None, :, :] * (block_len * (blocks - 1 - block_index))[:, None, None]
    )
    zero_row = zero_state[None, :, :]
    local_prev = jnp.concatenate([zero_row, inc_states[:-1]], axis=0)
    local_next = jnp.concatenate([inc_adj[1:], zero_row], axis=0)
    state_prev = local_prev + rise_power * carry_in[None, :, :]
    adj_next = local_next + fall_power * carry_back[None, :, :]
    out_table = weight_t[:, None, :] * powers * step_t[:, None, :]
    in_table = weight_t[:, None, :] * rev_powers * step_t[:, None, :]
    filtered = conv_local + jnp.sum(state_prev[:, :, None, :] * out_table[None, :, :, :], axis=1)
    back_filtered = back_local + jnp.sum(adj_next[:, :, None, :] * in_table[None, :, :, :], axis=1)
    filtered_rows = filtered.reshape(tok_rows, chan_count)
    back_rows = back_filtered.reshape(tok_rows, chan_count)
    grad_query = (grad_out.astype(jnp.float32) * filtered_rows).astype(jnp.bfloat16)
    grad_key = (back_rows * value_in.astype(jnp.float32)).astype(jnp.bfloat16)
    grad_value = (back_rows * key_in.astype(jnp.float32)).astype(jnp.bfloat16)
    raw_weight = intra_weight + step_t * jnp.sum(state_prev * start_adj, axis=0)
    cross_lag = (
        weighted_in * adj_next
        + weighted_out * state_prev
        + block_len * block_decay[None, :, :] * state_prev * adj_next
    )
    lag_total = intra_lag + step_t * jnp.sum(cross_lag, axis=0)
    raw_residue = (jnp.sqrt(2.0 * rate_t) * raw_weight).T
    raw_rate = (weight_t * (0.5 * raw_weight - rate_t * lag_total)).T
    summed_residue, summed_rate = lax.psum((raw_residue, raw_rate), "ctx")
    local_squares = jnp.sum(summed_residue * summed_residue) + jnp.sum(summed_rate * summed_rate)
    squares = lax.psum(local_squares, "tp")
    grad_scale = jnp.minimum(1.0, CLIP_NORM / jnp.sqrt(squares + 1e-06))
    residue_grad = summed_residue * grad_scale
    rate_grad = summed_rate * grad_scale
    return (grad_query, grad_key, grad_value, residue_grad, rate_grad)


def solution(mesh):
    in_specs = (
        P("ctx", "tp"),
        P("ctx", "tp"),
        P("ctx", "tp"),
        P("ctx", "tp"),
        P("tp", None),
        P("tp", None),
    )
    out_specs = (P("ctx", "tp"), P("ctx", "tp"), P("ctx", "tp"), P("tp", None), P("tp", None))
    return jax.shard_map(
        per_device, mesh=mesh, in_specs=in_specs, out_specs=out_specs, check_vma=False
    )
```

profile of v0, /device:TPU:0, one launch (start us, length us, event | category | flops | bytes accessed | tf_op | source)
XLA Modules:
  0.0 248.1 jit_solution(4231140041111939966)
XLA Ops:
  7.2 1.6 fusion.29
  8.9 1.0 fusion.25
  10.2 5.6 %rev.2 = f32[16,16,2048]{2,1,0:T(8,128)} reverse(f32[16,16,2048]{2,1,0:T(8,128)S(1)} %multiply_exponential_fusion), dimensions={1} | reverse | bytes 4194304 | tf_op jit(solution)/shard_map/rev | solution.py:41
  15.8 5.5 %multiply_multiply_fusion = (f32[16,16,2048]{2,1,0:T(8,128)}, f32[16,16,2048]{2,1,0:T(8,128)}, f32[16,16,2048]{2,1,0:T(8,128)}, f32[16,2048]{1,0:T(8,128)S(1)}, f32[16,16,2048]{2,1,0:T(8,128)}) fusion(f32[16,16,2048]{2,1,0:T(8,128)} %rev.2, f32[16,2048]{1,0:T(8,128)S(1)} %get-tuple-element.271, f32[16,2048]{1,0:T(8,128)S(1)} %get-tuple-element.272, ...), kind=kLoop, calls=%fused_computation.15 | loop fusion | flops 4161536 | bytes 11010112 | tf_op jit(solution)/shard_map/mul | solution.py:101
  21.3 1.0 fusion.21
  22.8 1.1 convert_multiply_fusion.1
  24.6 25.3 %multiply_reduce_fusion = (f32[8,16,2048]{2,1,0:T(8,128)}, f32[8,16,2048]{2,1,0:T(8,128)S(1)}, f32[8,16,2048]{2,1,0:T(8,128)S(1)}, f32[8,16,2048]{2,1,0:T(8,128)...) fusion(f32[16,16,2048]{2,1,0:T(8,128)} %get-tuple-element.267, ...), kind=kLoop, calls=%fused_computation.2 | loop fusion | flops 56623104 | bytes 20971520 | tf_op jit(solution)/shard_map/reduce_sum | solution.py:89
  51.4 2.6 %pad.99 = f32[7,16,2048]{2,1,0:T(8,128)} pad(f32[4,16,2048]{2,1,0:T(8,128)S(1)} %add.175, f32[]{:T(128)} %constant.88.clone.1), padding=0_0_1x0_0_0x0_0_0 | pad | bytes 1441796
  54.0 1.6 slice.276
  58.5 4.1 %pad.101 = f32[7,16,2048]{2,1,0:T(8,128)} pad(f32[4,16,2048]{2,1,0:T(8,128)} %add.186, f32[]{:T(128)} %constant.88.clone.1), padding=0_0_1x0_0_0x0_0_0 | pad | bytes 1441796
  62.7 1.6 slice.278
  64.3 2.1 fusion.8
  68.7 1.8 iota_multiply_fusion.1
  70.6 1.4 dynamic-slice
  72.7 2.0 pad.45
  74.6 23.1 %all-reduce.14 = f32[8]{0:T(128)S(1)} all-reduce(f32[8]{0:T(128)S(1)} %dynamic-update-slice), channel_id=1, replica_groups=mesh['ctx'=8,'tp'=4] {'ctx'}, use_global_device_ids=true, to_apply=%add.14 | all-reduce | flops 8 | bytes 64
  97.8 4.2 %pad.51 = f32[8,16,2048]{2,1,0:T(8,128)} pad(f32[4,16,2048]{2,1,0:T(8,128)} %add.186, f32[]{:T(128)} %constant.88.clone.1), padding=1_0_1x0_0_0x0_0_0 | pad | bytes 1572868 | tf_op jit(solution)/shard_map/pad | solution.py:63
  102.0 1.1 fusion.7
  104.0 4.1 %pad.50 = f32[8,16,2048]{2,1,0:T(8,128)} pad(f32[4,16,2048]{2,1,0:T(8,128)} %pad_maximum_fusion.1, f32[]{:T(128)} %constant.88.clone.1), padding=0_1_1x0_0_0x0_0_0 | pad | bytes 1572868 | tf_op jit(solution)/shard_map/pad | solution.py:63
  108.1 2.3 slice_add_fusion
  110.4 2.2 slice.188
  112.6 2.5 %multiply_reduce_fusion.9 = (f32[16,2048]{1,0:T(8,128)}, f32[16,2048]{1,0:T(8,128)}) fusion(f32[16,2048]{1,0:T(8,128)S(1)} %copy-done.28, f32[16,2048]{1,0:T(8,128)S(1)} %get-tuple-element.393, f32[16,2048]{1,0:T(8,128)} %get-tuple-element.275), kind=kLoop, calls=%fused_computation.13 | loop fusion | flops 2555904 | bytes 655360 | tf_op jit(solution)/shard_map/reduce_sum | solution.py:85
  116.0 2.0 pad.44
  118.0 1.0 slice_add_fusion.1
  119.0 21.0 %all-gather.5.cloned.1.call-done = f32[8,16,2048]{2,1,0:T(8,128)} async-done(((f32[1,16,2048]{2,1,0:T(8,128)}), f32[8,16,2048]{2,1,0:T(8,128)}) %all-gather.5.cloned.1.call-update) | async-done | bytes 1048592 | tf_op jit(solution)/shard_map/all_gather | solution.py:16
  140.0 15.9 %while.29 = (s32[]{:T(128)}, f32[16,2048]{1,0:T(8,128)S(1)}, s32[]{:T(128)}, f32[8]{0:T(128)S(1)}, f32[16,2048]{1,0:T(8,128)S(1)}, /*index=5*/f32[8,16,2048]{2,1...) while((s32[]{:T(128)}, f32[16,2048]{1,0:T(8,128)S(1)}, s32[]{:T(128)}, ...), condition=%wide.region_9.10_spmd, body=%wide.region_8.9_spmd.sunk | while | flops 98311 | bytes 524475 | solution.py:25
  156.0 4.6 %add_reduce_fusion = (f32[16,2048]{1,0:T(8,128)S(1)}, f32[16,2048]{1,0:T(8,128)S(1)}, f32[8,16,2048]{2,1,0:T(8,128)}, f32[8,16,2048]{2,1,0:T(8,128)}) fusion(f32[8,16,2048]{2,1,0:T(8,128)} %get-tuple-element.207, f32[8,16,2048]{2,1,0:T(8,128)} %get-tuple-element.210, f32[16,2048]{1,0:T(8,128)} %get-tuple-element.269, ...), kind=kLoop, calls=%fused_computation.28 | loop fusion | flops 3866624 | bytes 7864384 | tf_op jit(solution)/shard_map/reduce_sum | solution.py:115
  161.5 5.3 %multiply_reduce_fusion.3 = (f32[8,16,2048]{2,1,0:T(8,128)S(1)}, f32[8,16,2048]{2,1,0:T(8,128)S(1)}) fusion(f32[16,16,2048]{2,1,0:T(8,128)S(1)} %copy-done.1, f32[8,16,2048]{2,1,0:T(8,128)} %get-tuple-element.242, f32[16,16,2048]{2,1,0:T(8,128)} %get-tuple-element.261, f32[8,16,2048]{2,1,0:T(8,128)} %get-tuple-element.243), kind=kLoop, calls=%fused_computation.5 | loop fusion | flops 16252928 | bytes 8388608 | tf_op jit(solution)/shard_map/reduce_sum | solution.py:103
  168.0 1.3 fusion.4
  169.4 60.2 %all-reduce.18.cloned.1.call-done = (f32[2048,16]{0,1:T(8,128)}, f32[2048,16]{0,1:T(8,128)}) async-done(((f32[2048,16]{0,1:T(8,128)}, f32[2048,16]{0,1:T(8,128)}), (f32[2048,16]{0,1:T(8,128)}, f32[2048,16]{0,1:T(8,128)})) %all-reduce.18.cloned.1.call-update) | async-done | bytes 262160 | tf_op jit(solution)/shard_map/psum | solution.py:118
  229.5 1.7 multiply_reduce_fusion.12
  233.4 6.1 %psum.23 = f32[]{:T(128)} all-reduce(f32[]{:T(128)S(6)} %add.196), channel_id=1, replica_groups=mesh['ctx'=8,'tp'=4] {'tp'}, use_global_device_ids=true, to_apply=%region_22.23 | all-reduce | flops 1 | bytes 8 | tf_op jit(solution)/shard_map/psum | solution.py:120
  (126 shorter events, 26.0 us)
Async XLA Ops:
  7.2 111.8 %all-gather.3.cloned.1.call-start = ((), (), s32[]{:S(2)}) async-start(), calls=%async_computation | async-start | bytes 1179648 | tf_op jit(solution)/shard_map/all_gather | solution.py:16
  21.3 1.1 copy-start.20
  21.3 1.2 copy-start.25
  21.3 1.4 copy-start.16
  21.3 1.5 copy-start.18
  22.5 2.0 copy-start
  49.9 1.0 copy-start.3
  49.9 1.1 copy-start.14
  51.2 2.8 %copy-start.7 = (f32[4,16,2048]{2,1,0:T(8,128)}, f32[4,16,2048]{2,1,0:T(8,128)S(1)}, u32[]{:S(2)}) copy-start(f32[4,16,2048]{2,1,0:T(8,128)S(1)} %pad.43) | copy-start | bytes 1572868
  51.3 4.4 %copy-start.10 = (f32[4,16,2048]{2,1,0:T(8,128)}, f32[4,16,2048]{2,1,0:T(8,128)S(1)}, u32[]{:S(2)}) copy-start(f32[4,16,2048]{2,1,0:T(8,128)S(1)} %pad.42) | copy-start | bytes 1572868
  51.4 4.4 %copy-start.4 = (f32[4,16,2048]{2,1,0:T(8,128)}, f32[4,16,2048]{2,1,0:T(8,128)S(1)}, u32[]{:S(2)}) copy-start(f32[4,16,2048]{2,1,0:T(8,128)S(1)} %add.175) | copy-start | bytes 1572868
  55.6 84.4 %all-gather.5.cloned.1.call-start = ((), (), s32[]{:S(2)}) async-start(), calls=%async_computation.1 | async-start | bytes 1179648 | tf_op jit(solution)/shard_map/all_gather | solution.py:16
  58.5 10.2 %copy-start.2 = (f32[16,16,2048]{2,1,0:T(8,128)S(1)}, f32[16,16,2048]{2,1,0:T(8,128)}, u32[]{:S(2)}) copy-start(f32[16,16,2048]{2,1,0:T(8,128)} %get-tuple-element.211) | copy-start | bytes 6291460
  64.3 165.3 %all-reduce.18.cloned.1.call-start = ((), (), s32[]{:S(2)}) async-start(), calls=%async_computation.2 | async-start | bytes 524288 | tf_op jit(solution)/shard_map/psum | solution.py:118
  70.5 31.4 %copy-start.9 = (f32[4,16,2048]{2,1,0:T(8,128)S(1)}, f32[4,16,2048]{2,1,0:T(8,128)}, u32[]{:S(2)}) copy-start(f32[4,16,2048]{2,1,0:T(8,128)} %copy-done.8) | copy-start | bytes 1572868
  70.6 31.5 %copy-start.12 = (f32[4,16,2048]{2,1,0:T(8,128)S(1)}, f32[4,16,2048]{2,1,0:T(8,128)}, u32[]{:S(2)}) copy-start(f32[4,16,2048]{2,1,0:T(8,128)} %copy-done.11) | copy-start | bytes 1572868
  102.0 1.2 copy-start.26
  103.1 5.0 %copy-start.13 = (f32[8,16,2048]{2,1,0:T(8,128)S(1)}, f32[8,16,2048]{2,1,0:T(8,128)}, u32[]{:S(2)}) copy-start(f32[8,16,2048]{2,1,0:T(8,128)} %pad.51) | copy-start | bytes 3145732
  108.1 4.5 %copy-start.28 = (f32[16,2048]{1,0:T(8,128)S(1)}, f32[16,2048]{1,0:T(8,128)}, u32[]{:S(2)}) copy-start(f32[16,2048]{1,0:T(8,128)} %get-tuple-element.274) | copy-start | bytes 393220
  110.4 4.8 %copy-start.22 = (f32[3,16,2048]{2,1,0:T(8,128)S(1)}, f32[3,16,2048]{2,1,0:T(8,128)}, u32[]{:S(2)}) copy-start(f32[3,16,2048]{2,1,0:T(8,128)} %fusion.8) | copy-start | bytes 1179652
  156.0 4.6 %copy-start.15 = (f32[2048,16]{0,1:T(8,128)S(1)}, f32[2048,16]{0,1:T(8,128)}, u32[]{:S(2)}) copy-start(f32[2048,16]{0,1:T(8,128)} %param.15) | copy-start | bytes 393220
  156.0 4.6 %copy-start.27 = (f32[2048,16]{0,1:T(8,128)S(1)}, f32[2048,16]{0,1:T(8,128)}, u32[]{:S(2)}) copy-start(f32[2048,16]{0,1:T(8,128)} %param.14) | copy-start | bytes 393220
  156.0 4.6 %copy-start.29 = (f32[16,2048]{1,0:T(8,128)S(1)}, f32[16,2048]{1,0:T(8,128)}, u32[]{:S(2)}) copy-start(f32[16,2048]{1,0:T(8,128)} %get-tuple-element.214) | copy-start | bytes 393220
  156.0 4.6 %copy-start.30 = (f32[16,2048]{1,0:T(8,128)S(1)}, f32[16,2048]{1,0:T(8,128)}, u32[]{:S(2)}) copy-start(f32[16,2048]{1,0:T(8,128)} %get-tuple-element.215) | copy-start | bytes 393220
  156.0 5.4 %copy-start.1 = (f32[16,16,2048]{2,1,0:T(8,128)S(1)}, f32[16,16,2048]{2,1,0:T(8,128)}, u32[]{:S(2)}) copy-start(f32[16,16,2048]{2,1,0:T(8,128)} %get-tuple-element.244) | copy-start | bytes 6291460
  161.4 5.3 %copy-start.6 = (f32[8,16,2048]{2,1,0:T(8,128)S(1)}, f32[8,16,2048]{2,1,0:T(8,128)}, u32[]{:S(2)}) copy-start(f32[8,16,2048]{2,1,0:T(8,128)} %get-tuple-element.213) | copy-start | bytes 3145732
  166.8 1.0 copy-start.17
  166.8 1.2 copy-start.19
  168.0 1.3 copy-start.5
  169.2 63.3 %copy-start.21 = (bf16[128,2048]{1,0:T(8,128)(2,1)S(1)}, bf16[128,2048]{1,0:T(8,128)(2,1)}, u32[]{:S(2)}) copy-start(bf16[128,2048]{1,0:T(8,128)(2,1)} %param.10) | copy-start | bytes 1572868
  229.5 10.7 %copy-start.24 = (f32[2048,16]{0,1:T(8,128)S(1)}, f32[2048,16]{0,1:T(8,128)}, u32[]{:S(2)}) copy-start(f32[2048,16]{0,1:T(8,128)} %get-tuple-element.241) | copy-start | bytes 393220
  229.5 11.4 %copy-start.23 = (f32[2048,16]{0,1:T(8,128)S(1)}, f32[2048,16]{0,1:T(8,128)}, u32[]{:S(2)}) copy-start(f32[2048,16]{0,1:T(8,128)} %get-tuple-element.240) | copy-start | bytes 393220
  (2 other events, 1.6 us)
Sparse Core Ops, SparseCore 0:
  55.7 43.0 all-gather.2
  100.9 39.0 all-gather.4
  161.6 67.9 all-reduce.17
where the time goes:
time: 249 us; the launch traced here: 248 us
  waiting for transfers between devices  81.2 us (33%)
  other arithmetic  70.1 us (28%)
  local copies, waits for them, and re-layouts  43.5 us (17%)
  blocking collectives  29.3 us (12%)
  between operations  16.2 us (7%)
  loops' own time  4.94 us (2%)
  matrix products  2.83 us (1%)
    psum x1, waiting for transfers between devices, per_device(): summed_residue, summed_rate = lax.psum((raw_residue, raw_rate), 'ctx')  60.2 us
    reduce_sum x1, other arithmetic, per_device(): jnp.sum(gated_grad[:, None, :, :] * out_weights[None, :, :, :], axis=2)  25.3 us
    unnamed x1, blocking collectives  23.1 us
    all_gather x2, waiting for transfers between devices, entering(): gathered = jax.tree.map(lambda a: lax.all_gather(a, axis), part)  21 us
    unnamed x67, local copies, waits for them, and re-layouts  13.4 us
    pad x4, local copies, waits for them, and re-layouts, per_device(): lax.associative_scan(paired, (block_power, start_adj), axis=0, reverse=True)  8.42 us
    add x7, other arithmetic, counted(): return (earlier[0] + latter[0], span_decay * earlier[1] + latter[1])  6.87 us
    psum x1, blocking collectives, per_device(): squares = lax.psum(local_squares, 'tp')  6.14 us
  transfers between devices with their start and end apart: 3, of which 2 were waited for; matrix products, arithmetic and copies ran while one was open for 18% of the time, Pallas kernels for 0%

commit v1 on v0

v1 whole, which is shorter than its diff:
```python
import functools

import jax
import jax.numpy as jnp
from jax import lax
from jax.experimental import pallas as pl
from jax.experimental.pallas import tpu as pltpu
from jax.sharding import PartitionSpec as P

CLIP_NORM = 512
SUB = 8
LANES = 128
MESH = pl.DeviceIdType.MESH
VMEM_BYTES = 56 * 1024 * 1024


def shifted(x, by, row):
    moved = pltpu.roll(x, by % SUB, 0)
    keep = row >= by if by > 0 else row < SUB + by
    return jnp.where(keep, moved, 0.0)


def ends_kernel(rows, modes, go_ref, q_ref, k_ref, v_ref, lr_ref, ea_ref, sp_ref, an_ref, p_s, g_s):
    span = rows // SUB
    chunks = go_ref.shape[1] // LANES
    row = lax.broadcasted_iota(jnp.int32, (SUB, LANES), 0)

    def chunk(c, _):
        at = pl.ds(pl.multiple_of(c * LANES, LANES), LANES)
        p_s[...] = k_ref[:, at].astype(jnp.float32) * v_ref[:, at].astype(jnp.float32)
        g_s[...] = go_ref[:, at].astype(jnp.float32) * q_ref[:, at].astype(jnp.float32)
        rate = jnp.exp(lr_ref[:, at])
        decay = jnp.exp(-rate)
        steps = [jnp.exp(-rate * (span * n)) for n in (1, 2, 4)]
        for first in range(0, modes, 8):
            group = range(first, min(modes, first + 8))
            a = [jnp.broadcast_to(decay[m : m + 1], (SUB, LANES)) for m in group]
            s = [jnp.zeros((SUB, LANES), jnp.float32)] * len(a)
            for i in range(span):
                x = p_s[pl.ds(i, SUB, stride=span), :]
                s = [aa * ss + x for aa, ss in zip(a, s)]
            t = [jnp.zeros((SUB, LANES), jnp.float32)] * len(a)
            for i in reversed(range(span)):
                x = g_s[pl.ds(i, SUB, stride=span), :]
                t = [aa * tt + x for aa, tt in zip(a, t)]
            for at_m, m in enumerate(group):
                x, y = s[at_m], t[at_m]
                for n, table in zip((1, 2, 4), steps):
                    power = jnp.broadcast_to(table[m : m + 1], (SUB, LANES))
                    x = x + power * shifted(x, n, row)
                    y = y + power * shifted(y, -n, row)
                sp_ref[m, :, at] = shifted(x, 1, row)
                an_ref[m, :, at] = shifted(y, -1, row)
                ea_ref[0, m : m + 1, at] = x[SUB - 1 : SUB]
                ea_ref[1, m : m + 1, at] = y[0:1]
        return 0

    lax.fori_loop(0, chunks, chunk, 0)


def carry_kernel(n, rows, ea_ref, lr_ref, out_ref, held, send_sem, recv_sem):
    me = lax.axis_index("ctx")
    barrier = pltpu.get_barrier_semaphore()
    for k in range(1, n):
        pl.semaphore_signal(
            barrier, inc=1, device_id={"ctx": lax.rem(me + k, n)}, device_id_type=MESH
        )
    pl.semaphore_wait(barrier, n - 1)
    copies = []
    for k in range(1, n):
        there = lax.rem(me + k, n)
        which = jnp.where(there < me, 1, 0)
        copy = pltpu.make_async_remote_copy(
            src_ref=ea_ref.at[which],
            dst_ref=held.at[k - 1],
            send_sem=send_sem.at[k - 1],
            recv_sem=recv_sem.at[k - 1],
            device_id={"ctx": there},
            device_id_type=MESH,
        )
        copy.start()
        copies.append(copy)
    rate = jnp.exp(lr_ref[...])
    out_ref[...] = jnp.zeros_like(out_ref)
    for k in range(1, n):
        copies[k - 1].wait_recv()
        origin = lax.rem(me - k + n, n)
        which = jnp.where(origin < me, 0, 1)
        gap = jnp.where(origin < me, me - origin, origin - me) - 1
        power = jnp.exp(-rate * (gap * rows).astype(jnp.float32))
        out_ref[which] += power * held[k - 1]
    for copy in copies:
        copy.wait_send()


def main_kernel(
    rows, modes, go_ref, q_ref, k_ref, v_ref, lr_ref, res_ref, ca_ref, sp_ref, an_ref,
    gq_ref, gk_ref, gv_ref, w_ref, p_s, g_s, f_s, b_s, s_s, fr_s, br_s,
):
    span = rows // SUB
    chunks = go_ref.shape[1] // LANES
    row = lax.broadcasted_iota(jnp.int32, (SUB, LANES), 0).astype(jnp.float32)
    size = 4

    def chunk(c, _):
        at = pl.ds(pl.multiple_of(c * LANES, LANES), LANES)
        p_s[...] = k_ref[:, at].astype(jnp.float32) * v_ref[:, at].astype(jnp.float32)
        g_s[...] = go_ref[:, at].astype(jnp.float32) * q_ref[:, at].astype(jnp.float32)
        rate = jnp.exp(lr_ref[:, at])
        decay = jnp.exp(-rate)
        root = jnp.sqrt(2.0 * rate)
        weight = res_ref[:, at] * root
        carry_in = ca_ref[0, :, at]
        carry_back = ca_ref[1, :, at]
        wide = lambda x, m: jnp.broadcast_to(x[m : m + 1], (SUB, LANES))
        raw, lag = [], []
        for first in range(0, modes, size):
            group = range(first, first + size)
            a = [wide(decay, m) for m in group]
            w = [wide(weight, m) for m in group]
            s = [
                sp_ref[m, :, at] + jnp.exp(-wide(rate, m) * (span * row)) * wide(carry_in, m)
                for m in group
            ]
            t = [
                an_ref[m, :, at]
                + jnp.exp(-wide(rate, m) * (span * (SUB - 1 - row))) * wide(carry_back, m)
                for m in group
            ]
            rw = [jnp.zeros((SUB, LANES), jnp.float32)] * size
            lg = [jnp.zeros((SUB, LANES), jnp.float32)] * size
            for i in range(span):
                x = p_s[pl.ds(i, SUB, stride=span), :]
                y = g_s[pl.ds(i, SUB, stride=span), :]
                s = [aa * ss + x for aa, ss in zip(a, s)]
                for j in range(size):
                    s_s[i * size + j] = s[j]
                rw = [r + y * ss for r, ss in zip(rw, s)]
                f = (w[0] * s[0] + w[1] * s[1]) + (w[2] * s[2] + w[3] * s[3])
                if first == 0:
                    f_s[i] = f
                elif first + size < modes:
                    f_s[i] += f
                else:
                    fr_s[pl.ds(i, SUB, stride=span), :] = f_s[i] + f
            for i in reversed(range(span)):
                y = g_s[pl.ds(i, SUB, stride=span), :]
                lg = [l + s_s[i * size + j] * t[j] for j, l in enumerate(lg)]
                t = [aa * tt + y for aa, tt in zip(a, t)]
                b = (w[0] * t[0] + w[1] * t[1]) + (w[2] * t[2] + w[3] * t[3])
                if first == 0:
                    b_s[i] = b
                elif first + size < modes:
                    b_s[i] += b
                else:
                    br_s[pl.ds(i, SUB, stride=span), :] = b_s[i] + b
            raw += [jnp.sum(r, axis=0, keepdims=True) for r in rw]
            lag += [jnp.sum(l, axis=0, keepdims=True) for l in lg]
        gq_ref[:, at] = (go_ref[:, at].astype(jnp.float32) * fr_s[...]).astype(jnp.bfloat16)
        back = br_s[...]
        gk_ref[:, at] = (back * v_ref[:, at].astype(jnp.float32)).astype(jnp.bfloat16)
        gv_ref[:, at] = (back * k_ref[:, at].astype(jnp.float32)).astype(jnp.bfloat16)
        raw_weight = jnp.concatenate(raw, axis=0)
        lag_total = decay * jnp.concatenate(lag, axis=0)
        w_ref[c, 0:modes] = root * raw_weight
        w_ref[c, modes : 2 * modes] = weight * (0.5 * raw_weight - rate * lag_total)
        return 0

    lax.fori_loop(0, chunks, chunk, 0)


def clip_kernel(n, ntp, g_ref, out_ref, held, red, gath, squares, send_sem, recv_sem, sq_send, sq_recv):
    me = lax.axis_index("ctx")
    lane = lax.axis_index("tp")
    total = n * ntp
    here = me * ntp + lane
    tiles = g_ref.shape[0] // n
    barrier = pltpu.get_barrier_semaphore()

    def place(q):
        other = lax.rem(here + q, total)
        return {"ctx": other // ntp, "tp": lax.rem(other, ntp)}

    def greet(q, _):
        pl.semaphore_signal(barrier, inc=1, device_id=place(q), device_id_type=MESH)
        return 0

    lax.fori_loop(1, total, greet, 0)
    pl.semaphore_wait(barrier, total - 1)

    def send(phase, src, dst, k):
        copy = pltpu.make_async_remote_copy(
            src_ref=src,
            dst_ref=dst,
            send_sem=send_sem.at[phase, k - 1],
            recv_sem=recv_sem.at[phase, k - 1],
            device_id={"ctx": lax.rem(me + k, n)},
            device_id_type=MESH,
        )
        copy.start()
        return copy

    first = []
    for k in range(1, n):
        there = lax.rem(me + k, n)
        first.append(send(0, g_ref.at[pl.ds(there * tiles, tiles)], held.at[k - 1], k))
    mine = g_ref[pl.ds(me * tiles, tiles)]
    for k in range(1, n):
        first[k - 1].wait_recv()
        mine = mine + held[k - 1]
    red[...] = mine
    squares[here] = jnp.sum(mine * mine, axis=0)

    def sq_copy(q):
        return pltpu.make_async_remote_copy(
            src_ref=squares.at[here],
            dst_ref=squares.at[here],
            send_sem=sq_send.at[q - 1],
            recv_sem=sq_recv.at[q - 1],
            device_id=place(q),
            device_id_type=MESH,
        )

    def sq_start(q, _):
        sq_copy(q).start()
        return 0

    lax.fori_loop(1, total, sq_start, 0)
    second = [send(1, red, gath.at[pl.ds(me * tiles, tiles)], k) for k in range(1, n)]
    gath[pl.ds(me * tiles, tiles)] = mine

    def sq_wait(q, _):
        sq_copy(q).wait()
        return 0

    lax.fori_loop(1, total, sq_wait, 0)
    norm = jnp.sum(jnp.sum(squares[...], axis=0), keepdims=True)
    scale = jnp.minimum(1.0, CLIP_NORM / jnp.sqrt(norm + 1e-06))
    for copy in second:
        copy.wait_recv()
    out_ref[...] = gath[...] * scale
    for copy in first + second:
        copy.wait_send()


def per_device(n, ntp, grad_out, query_in, key_in, value_in, residue, log_rate):
    rows, chans = grad_out.shape
    modes = residue.shape[1]
    span = rows // SUB
    chunks = chans // LANES
    f32 = jnp.float32
    shape = jax.ShapeDtypeStruct
    vmem = pl.BlockSpec(memory_space=pltpu.VMEM)
    rate_t = log_rate.T
    res_t = residue.T
    data = (grad_out, query_in, key_in, value_in)
    tile = lambda *lead: pltpu.VMEM((*lead, SUB, LANES), f32)
    flat = pltpu.VMEM((rows, LANES), f32)
    ends, sprev, anext = pl.pallas_call(
        functools.partial(ends_kernel, rows, modes),
        out_shape=(
            shape((2, modes, chans), f32),
            shape((modes, SUB, chans), f32),
            shape((modes, SUB, chans), f32),
        ),
        in_specs=[vmem] * 5,
        out_specs=(vmem,) * 3,
        scratch_shapes=[flat, flat],
        compiler_params=pltpu.CompilerParams(vmem_limit_bytes=VMEM_BYTES),
        name="ends",
    )(*data, rate_t)
    carries = pl.pallas_call(
        functools.partial(carry_kernel, n, rows),
        out_shape=shape((2, modes, chans), f32),
        in_specs=[vmem] * 2,
        out_specs=vmem,
        scratch_shapes=[
            pltpu.VMEM((n - 1, modes, chans), f32),
            pltpu.SemaphoreType.DMA((n - 1,)),
            pltpu.SemaphoreType.DMA((n - 1,)),
        ],
        compiler_params=pltpu.CompilerParams(
            collective_id=0, has_side_effects=True, vmem_limit_bytes=VMEM_BYTES
        ),
        name="carry",
    )(ends, rate_t)
    grad_query, grad_key, grad_value, raw = pl.pallas_call(
        functools.partial(main_kernel, rows, modes),
        out_shape=(shape((rows, chans), jnp.bfloat16),) * 3
        + (shape((chunks, 2 * modes, LANES), f32),),
        in_specs=[vmem] * 9,
        out_specs=(vmem,) * 4,
        scratch_shapes=[flat, flat, tile(span), tile(span), tile(4 * span), flat, flat],
        compiler_params=pltpu.CompilerParams(vmem_limit_bytes=VMEM_BYTES),
        name="main",
    )(*data, rate_t, res_t, carries, sprev, anext)
    used = chunks * 2 * modes // SUB
    count = -(-used // n) * n
    raw = raw.reshape(used, SUB, LANES)
    if count > used:
        raw = jnp.pad(raw, ((0, count - used), (0, 0), (0, 0)))
    clipped = pl.pallas_call(
        functools.partial(clip_kernel, n, ntp),
        out_shape=shape((count, SUB, LANES), f32),
        in_specs=[vmem],
        out_specs=vmem,
        scratch_shapes=[
            tile(n - 1, count // n),
            tile(count // n),
            tile(count),
            tile(n * ntp),
            pltpu.SemaphoreType.DMA((2, n - 1)),
            pltpu.SemaphoreType.DMA((2, n - 1)),
            pltpu.SemaphoreType.DMA((n * ntp - 1,)),
            pltpu.SemaphoreType.DMA((n * ntp - 1,)),
        ],
        compiler_params=pltpu.CompilerParams(
            collective_id=1, has_side_effects=True, vmem_limit_bytes=VMEM_BYTES
        ),
        name="clip",
    )(raw)
    grads = clipped[:used].reshape(chunks, 2, modes, LANES).transpose(1, 0, 3, 2)
    grads = grads.reshape(2, chans, modes)
    return grad_query, grad_key, grad_value, grads[0], grads[1]


def solution(mesh):
    wide = P("ctx", "tp")
    tall = P("tp", None)
    body = functools.partial(per_device, mesh.shape["ctx"], mesh.shape["tp"])
    return jax.shard_map(
        body,
        mesh=mesh,
        in_specs=(wide,) * 4 + (tall,) * 2,
        out_specs=(wide,) * 3 + (tall,) * 2,
        check_vma=False,
    )
```

time: 249 us -> 77.3 us (0.31)
  waiting for transfers between devices: 81.2 us -> 0 us
  Pallas kernels: 0 us -> 74.6 us
  other arithmetic: 70.1 us -> 0 us
  local copies, waits for them, and re-layouts: 43.5 us -> 1.87 us
  blocking collectives: 29.3 us -> 0 us
  between operations: 16.2 us -> 0.67 us
  loops' own time: 4.94 us -> 0 us
  matrix products: 2.83 us -> 0 us
    pallas_call x0 -> x4, Pallas kernels: none -> 74.6 us  [the longest x1 28.4 us: per_device(): pl.pallas_call(functools.partial(clip_kernel, n, ntp), out_shape=shape((c...]
    psum x1 -> x0, waiting for transfers between devices: 60.2 us -> none  [per_device(): summed_residue, summed_rate = lax.psum((raw_residue, raw_rate), 'ctx')]
    reduce_sum x5 -> x0, other arithmetic: 39.3 us -> none  [the longest x1 25.3 us: per_device(): jnp.sum(gated_grad[:, None, :, :] * out_weights[None, :, :, :], axis=2)]
    unnamed x1 -> x0, blocking collectives: 23.1 us -> none
    all_gather x2 -> x0, waiting for transfers between devices: 21 us -> none  [entering(): gathered = jax.tree.map(lambda a: lax.all_gather(a, axis), part)]
    add x19 -> x0, other arithmetic: 14.6 us -> none  [the longest x7 6.87 us: counted(): return (earlier[0] + latter[0], span_decay * earlier[1] + latter[1])]
    unnamed x67 -> x0, local copies, waits for them, and re-layouts: 13.4 us -> none
    pad x8 -> x0, local copies, waits for them, and re-layouts: 12.5 us -> none  [the longest x4 8.42 us: per_device(): lax.associative_scan(paired, (block_power, start_adj), axis=0, reverse=True)]
  transfers between devices with their start and end apart: 3 -> 0, of which waited for: 2 -> 0; matrix products, arithmetic and copies ran while one was open for 18% -> 0% of each run, Pallas kernels for 0% -> 0%
where the time goes in v1:
time: 77.3 us; the launch traced here: 77.1 us
  Pallas kernels  74.6 us (97%)
  local copies, waits for them, and re-layouts  1.87 us (2%)
    pallas_call x1, Pallas kernels, per_device(): pl.pallas_call(functools.partial(clip_kernel, n, ntp), out_shape=shape((c...  28.4 us
    pallas_call x1, Pallas kernels, per_device(): pl.pallas_call(functools.partial(carry_kernel, n, rows), out_shape=shape(...  24.7 us
    pallas_call x1, Pallas kernels, per_device(): pl.pallas_call(functools.partial(main_kernel, rows, modes), out_shape=(sh...  14 us
    pallas_call x1, Pallas kernels, per_device(): pl.pallas_call(functools.partial(ends_kernel, rows, modes), out_shape=(sh...  7.5 us

profile of v1, /device:TPU:0, one launch (start us, length us, event | category | flops | bytes accessed | tf_op | source)
XLA Modules:
  0.0 77.1 jit_solution(2018576239664062189)
XLA Ops:
  0.6 7.5 %ends.1 = (f32[2,16,2048]{2,1,0:T(8,128)}, f32[16,8,2048]{2,1,0:T(8,128)}, f32[16,8,2048]{2,1,0:T(8,128)}) custom-call(bf16[128,2048]{1,0:T(8,128)(2,1)} %go_ref.3, bf16[128,2048]{1,0:T(8,128)(2,1)} %q_ref.3, bf16[128,2048]{1,0:T(8,128)(2,1)} %k_ref.3, bf16[128,2048]{1,0:T(8,128)(2,1)} %v_ref.3, f32[16,2048]{1,0:T(8,128)} %bitcast.18), custom_call_target="tpu_custom_call" | custom-call | tf_op jit(solution)/shard_map/ends/pallas_call | solution.py:259
  8.1 24.7 %carry.1.ca_ref = f32[2,16,2048]{2,1,0:T(8,128)} custom-call(f32[2,16,2048]{2,1,0:T(8,128)} %get-tuple-element.12.ea_ref, f32[16,2048]{1,0:T(8,128)} %bitcast.19), custom_call_target="tpu_custom_call" | custom-call | tf_op jit(solution)/shard_map/carry/pallas_call | solution.py:272
  32.8 14.0 %main.1 = (bf16[128,2048]{1,0:T(8,128)(2,1)}, bf16[128,2048]{1,0:T(8,128)(2,1)}, bf16[128,2048]{1,0:T(8,128)(2,1)}, f32[16,32,128]{2,1,0:T(8,128)}) custom-call(bf16[128,2048]{1,0:T(8,128)(2,1)} %go_ref.3, bf16[128,2048]{1,0:T(8,128)(2,1)} %q_ref.3, bf16[128,2048]{1,0:T(8,128)(2,1)} %k_ref.3, bf16[128,2048]{1,0:T(8,128)(2,1)} %v_ref.3, f32[16,2048]{1,0:T(8,128)} %bitcast.20, ...), custom_call_target="tpu_custom_call" | custom-call | tf_op jit(solution)/shard_map/main/pallas_call | solution.py:287
  46.8 28.4 %clip.1 = f32[64,8,128]{2,1,0:T(8,128)} custom-call(f32[64,8,128]{2,1,0:T(8,128)} %bitcast.24), custom_call_target="tpu_custom_call" | custom-call | tf_op jit(solution)/shard_map/clip/pallas_call | solution.py:302
  75.2 1.0 %fusion = (f32[1,16,128,16]{2,3,0,1:T(8,128)S(1)}, f32[1,16,128,16]{2,3,0,1:T(8,128)S(1)}) fusion(f32[2,16,128,16]{2,3,0,1:T(8,128)} %bitcast.21), kind=kLoop, calls=%fused_computation.2 | loop fusion | bytes 524288 | tf_op jit(solution)/shard_map/slice | solution.py:324
  76.3 0.8 %copy_bitcast_fusion = (f32[2048,16]{0,1:T(8,128)}, f32[2048,16]{0,1:T(8,128)}) fusion(f32[2,8,16,128]{3,2,1,0:T(8,128)S(1)} %bitcast.22, f32[2,8,16,128]{3,2,1,0:T(8,128)S(1)} %bitcast.23), kind=kLoop, calls=%fused_computation | loop fusion | bytes 524288 | tf_op jit(solution)/shard_map/squeeze | solution.py:324
  (2 shorter events, 0.1 us)

commit v2 on v0

v2 whole, which is shorter than its diff:
```python
import functools

import jax
import jax.numpy as jnp
from jax import lax
from jax.experimental import pallas as pl
from jax.experimental.pallas import tpu as pltpu
from jax.sharding import PartitionSpec as P

CLIP_NORM = 512
SUB = 8
LANES = 128
MESH = pl.DeviceIdType.MESH
VMEM_BYTES = 56 * 1024 * 1024


def shifted(x, by, row):
    moved = pltpu.roll(x, by % SUB, 0)
    keep = row >= by if by > 0 else row < SUB + by
    return jnp.where(keep, moved, 0.0)


def fused_kernel(
    n, ntp, modes, groups,
    go_ref, q_ref, k_ref, v_ref, lr_ref, res_ref,
    gq_ref, gk_ref, gv_ref, dres_ref, drate_ref,
    p_s, g_s, f_s, b_s, s_s, fr_s, br_s, sp_s, an_s,
    ea_s, held, ca_s, raw_s, parts, red, gath, squares,
    ex_send, ex_recv, rs_send, rs_recv, ag_send, ag_recv, sq_send, sq_recv,
):
    me = lax.axis_index("ctx")
    total = n * ntp
    here = me * ntp + lax.axis_index("tp")
    rows, chans = go_ref.shape
    span = rows // SUB
    per_group = chans // groups // LANES
    pieces = 2 * modes // SUB
    own = raw_s.shape[1] // n
    row = lax.broadcasted_iota(jnp.int32, (SUB, LANES), 0)
    level = row.astype(jnp.float32)
    zero = jnp.zeros((SUB, LANES), jnp.float32)
    size = 4

    def place(q):
        other = lax.rem(here + q, total)
        return {"ctx": other // ntp, "tp": lax.rem(other, ntp)}

    def peer(k):
        return {"ctx": lax.rem(me + k, n)}

    barrier = pltpu.get_barrier_semaphore()

    def greet(q, _):
        pl.semaphore_signal(barrier, inc=1, device_id=place(q), device_id_type=MESH)
        return 0

    lax.fori_loop(1, total, greet, 0)

    def wide(x, m):
        return jnp.broadcast_to(x[m : m + 1], (SUB, LANES))

    def gates(at):
        p_s[...] = k_ref[:, at].astype(jnp.float32) * v_ref[:, at].astype(jnp.float32)
        g_s[...] = go_ref[:, at].astype(jnp.float32) * q_ref[:, at].astype(jnp.float32)

    def places(g, c):
        at = pl.ds(pl.multiple_of((g * per_group + c) * LANES, LANES), LANES)
        return at, pl.ds(pl.multiple_of(c * LANES, LANES), LANES)

    def ends(g):
        def chunk(c, _):
            at, inner = places(g, c)
            gates(at)
            rate = jnp.exp(lr_ref[:, at])
            decay = jnp.exp(-rate)
            steps = [jnp.exp(-rate * (span * far)) for far in (1, 2, 4)]
            for first in range(0, modes, 8):
                group = range(first, min(modes, first + 8))
                a = [wide(decay, m) for m in group]
                s = [zero] * len(a)
                for i in range(span):
                    x = p_s[pl.ds(i, SUB, stride=span), :]
                    s = [aa * ss + x for aa, ss in zip(a, s)]
                t = [zero] * len(a)
                for i in reversed(range(span)):
                    x = g_s[pl.ds(i, SUB, stride=span), :]
                    t = [aa * tt + x for aa, tt in zip(a, t)]
                for slot, m in enumerate(group):
                    x, y = s[slot], t[slot]
                    for far, table in zip((1, 2, 4), steps):
                        power = wide(table, m)
                        x = x + power * shifted(x, far, row)
                        y = y + power * shifted(y, -far, row)
                    sp_s[m, :, at] = shifted(x, 1, row)
                    an_s[m, :, at] = shifted(y, -1, row)
                    ea_s[g, 0, m : m + 1, inner] = x[SUB - 1 : SUB]
                    ea_s[g, 1, m : m + 1, inner] = y[0:1]
            return 0

        lax.fori_loop(0, per_group, chunk, 0)

    def exchange(g, k):
        which = jnp.where(lax.rem(me + k, n) < me, 1, 0)
        return pltpu.make_async_remote_copy(
            src_ref=ea_s.at[g, which],
            dst_ref=held.at[g, k - 1],
            send_sem=ex_send.at[g, k - 1],
            recv_sem=ex_recv.at[g, k - 1],
            device_id=peer(k),
            device_id_type=MESH,
        )

    def scatter(g, k):
        there = lax.rem(me + k, n)
        return pltpu.make_async_remote_copy(
            src_ref=raw_s.at[g, pl.ds(there * own, own)],
            dst_ref=parts.at[g, k - 1],
            send_sem=rs_send.at[g, k - 1],
            recv_sem=rs_recv.at[g, k - 1],
            device_id=peer(k),
            device_id_type=MESH,
        )

    def gather(k):
        return pltpu.make_async_remote_copy(
            src_ref=red,
            dst_ref=gath.at[me],
            send_sem=ag_send.at[k - 1],
            recv_sem=ag_recv.at[k - 1],
            device_id=peer(k),
            device_id_type=MESH,
        )

    def norm(q):
        return pltpu.make_async_remote_copy(
            src_ref=squares.at[here],
            dst_ref=squares.at[here],
            send_sem=sq_send.at[q - 1],
            recv_sem=sq_recv.at[q - 1],
            device_id=place(q),
            device_id_type=MESH,
        )

    def carry(g):
        at = pl.ds(pl.multiple_of(g * per_group * LANES, LANES), per_group * LANES)
        rate = jnp.exp(lr_ref[:, at])
        ca_s[...] = jnp.zeros_like(ca_s)
        for k in range(1, n):
            exchange(g, k).wait_recv()
            origin = lax.rem(me - k + n, n)
            which = jnp.where(origin < me, 0, 1)
            gap = jnp.where(origin < me, me - origin, origin - me) - 1
            power = jnp.exp(-rate * (gap * rows).astype(jnp.float32))
            ca_s[which] += power * held[g, k - 1]

    def main(g):
        def chunk(c, _):
            at, inner = places(g, c)
            gates(at)
            rate = jnp.exp(lr_ref[:, at])
            decay = jnp.exp(-rate)
            root = jnp.sqrt(2.0 * rate)
            weight = res_ref[:, at] * root
            carry_in = ca_s[0, :, inner]
            carry_back = ca_s[1, :, inner]
            raw, lag = [], []
            for first in range(0, modes, size):
                group = range(first, first + size)
                a = [wide(decay, m) for m in group]
                w = [wide(weight, m) for m in group]
                s = [
                    sp_s[m, :, at]
                    + jnp.exp(-wide(rate, m) * (span * level)) * wide(carry_in, m)
                    for m in group
                ]
                t = [
                    an_s[m, :, at]
                    + jnp.exp(-wide(rate, m) * (span * (SUB - 1 - level))) * wide(carry_back, m)
                    for m in group
                ]
                rw = [zero] * size
                lg = [zero] * size
                for i in range(span):
                    x = p_s[pl.ds(i, SUB, stride=span), :]
                    y = g_s[pl.ds(i, SUB, stride=span), :]
                    s = [aa * ss + x for aa, ss in zip(a, s)]
                    for j in range(size):
                        s_s[i * size + j] = s[j]
                    rw = [r + y * ss for r, ss in zip(rw, s)]
                    f = (w[0] * s[0] + w[1] * s[1]) + (w[2] * s[2] + w[3] * s[3])
                    if first == 0:
                        f_s[i] = f
                    elif first + size < modes:
                        f_s[i] += f
                    else:
                        fr_s[pl.ds(i, SUB, stride=span), :] = f_s[i] + f
                for i in reversed(range(span)):
                    y = g_s[pl.ds(i, SUB, stride=span), :]
                    lg = [l + s_s[i * size + j] * t[j] for j, l in enumerate(lg)]
                    t = [aa * tt + y for aa, tt in zip(a, t)]
                    b = (w[0] * t[0] + w[1] * t[1]) + (w[2] * t[2] + w[3] * t[3])
                    if first == 0:
                        b_s[i] = b
                    elif first + size < modes:
                        b_s[i] += b
                    else:
                        br_s[pl.ds(i, SUB, stride=span), :] = b_s[i] + b
                raw += [jnp.sum(r, axis=0, keepdims=True) for r in rw]
                lag += [jnp.sum(l, axis=0, keepdims=True) for l in lg]
            gq_ref[:, at] = (go_ref[:, at].astype(jnp.float32) * fr_s[...]).astype(jnp.bfloat16)
            back = br_s[...]
            gk_ref[:, at] = (back * v_ref[:, at].astype(jnp.float32)).astype(jnp.bfloat16)
            gv_ref[:, at] = (back * k_ref[:, at].astype(jnp.float32)).astype(jnp.bfloat16)
            raw_weight = jnp.concatenate(raw, axis=0)
            lag_total = decay * jnp.concatenate(lag, axis=0)
            both = (root * raw_weight, weight * (0.5 * raw_weight - rate * lag_total))
            for piece in range(pieces):
                low = piece % (pieces // 2) * SUB
                raw_s[g, c * pieces + piece] = both[piece // (pieces // 2)][low : low + SUB]
            return 0

        lax.fori_loop(0, per_group, chunk, 0)

    if raw_s.shape[1] > per_group * pieces:
        raw_s[...] = jnp.zeros_like(raw_s)

    def first_stage(g, _):
        ends(g)
        for k in range(1, n):
            exchange(g, k).start()
        return 0

    def second_stage(g, _):
        carry(g)
        main(g)
        for k in range(1, n):
            scatter(g, k).start()
        return 0

    ends(0)
    pl.semaphore_wait(barrier, total - 1)
    for k in range(1, n):
        exchange(0, k).start()
    lax.fori_loop(1, groups, first_stage, 0)
    lax.fori_loop(0, groups, second_stage, 0)

    sums = zero
    for g in range(groups):
        mine = raw_s[g, pl.ds(me * own, own)]
        for k in range(1, n):
            scatter(g, k).wait_recv()
            mine = mine + parts[g, k - 1]
        red[g] = mine
        sums = sums + jnp.sum(mine * mine, axis=0)
    squares[here] = sums

    def norm_start(q, _):
        norm(q).start()
        return 0

    lax.fori_loop(1, total, norm_start, 0)
    for k in range(1, n):
        gather(k).start()
    gath[me] = red[...]

    def norm_wait(q, _):
        norm(q).wait()
        return 0

    lax.fori_loop(1, total, norm_wait, 0)
    square = jnp.sum(jnp.sum(squares[...], axis=0), keepdims=True)
    scale = jnp.minimum(1.0, CLIP_NORM / jnp.sqrt(square + 1e-06))
    for k in range(1, n):
        gather(k).wait_recv()
    for g in range(groups):
        for c in range(per_group):
            at = pl.ds((g * per_group + c) * LANES, LANES)
            for piece in range(pieces):
                tile = c * pieces + piece
                low = piece % (pieces // 2) * SUB
                ref = dres_ref if piece < pieces // 2 else drate_ref
                ref[low : low + SUB, at] = gath[tile // own, g, tile % own] * scale

    def drain(g, _):
        for k in range(1, n):
            exchange(g, k).wait_send()
            scatter(g, k).wait_send()
        return 0

    lax.fori_loop(0, groups, drain, 0)
    for k in range(1, n):
        gather(k).wait_send()


def per_device(n, ntp, grad_out, query_in, key_in, value_in, residue, log_rate):
    rows, chans = grad_out.shape
    modes = residue.shape[1]
    span = rows // SUB
    chunks = chans // LANES
    groups = 4 if chunks % 4 == 0 and n <= 32 else 1
    width = chans // groups
    own = -(-(width // LANES * 2 * modes // SUB) // n)
    f32 = jnp.float32
    shape = jax.ShapeDtypeStruct
    vmem = pl.BlockSpec(memory_space=pltpu.VMEM)
    buffer = lambda *dims: pltpu.VMEM(dims, f32)
    tile = lambda *lead: pltpu.VMEM((*lead, SUB, LANES), f32)
    flags = lambda *dims: pltpu.SemaphoreType.DMA(dims)
    flat = buffer(rows, LANES)
    wide_out = shape((rows, chans), jnp.bfloat16)
    tall_out = shape((modes, chans), f32)
    grad_query, grad_key, grad_value, d_res, d_rate = pl.pallas_call(
        functools.partial(fused_kernel, n, ntp, modes, groups),
        out_shape=(wide_out,) * 3 + (tall_out,) * 2,
        in_specs=[vmem] * 6,
        out_specs=(vmem,) * 5,
        scratch_shapes=[
            flat, flat, tile(span), tile(span), tile(4 * span), flat, flat,
            buffer(modes, SUB, chans),
            buffer(modes, SUB, chans),
            buffer(groups, 2, modes, width),
            buffer(groups, n - 1, modes, width),
            buffer(2, modes, width),
            tile(groups, own * n),
            tile(groups, n - 1, own),
            tile(groups, own),
            tile(n, groups, own),
            tile(n * ntp),
            flags(groups, n - 1), flags(groups, n - 1),
            flags(groups, n - 1), flags(groups, n - 1),
            flags(n - 1), flags(n - 1),
            flags(n * ntp - 1), flags(n * ntp - 1),
        ],
        compiler_params=pltpu.CompilerParams(
            collective_id=0, has_side_effects=True, vmem_limit_bytes=VMEM_BYTES
        ),
        name="fused",
    )(grad_out, query_in, key_in, value_in, log_rate.T, residue.T)
    return grad_query, grad_key, grad_value, d_res.T, d_rate.T


def solution(mesh):
    wide = P("ctx", "tp")
    tall = P("tp", None)
    body = functools.partial(per_device, mesh.shape["ctx"], mesh.shape["tp"])
    return jax.shard_map(
        body,
        mesh=mesh,
        in_specs=(wide,) * 4 + (tall,) * 2,
        out_specs=(wide,) * 3 + (tall,) * 2,
        check_vma=False,
    )
```

time: 249 us -> 59.4 us (0.24)
  waiting for transfers between devices: 81.2 us -> 0 us
  other arithmetic: 70.1 us -> 0 us
  Pallas kernels: 0 us -> 52.6 us
  local copies, waits for them, and re-layouts: 43.5 us -> 5.8 us
  blocking collectives: 29.3 us -> 0 us
  between operations: 16.2 us -> 0.65 us
  loops' own time: 4.94 us -> 0 us
  matrix products: 2.83 us -> 0 us
    psum x1 -> x0, waiting for transfers between devices: 60.2 us -> none  [per_device(): summed_residue, summed_rate = lax.psum((raw_residue, raw_rate), 'ctx')]
    pallas_call x0 -> x1, Pallas kernels: none -> 52.6 us  [per_device(): pl.pallas_call(functools.partial(fused_kernel, n, ntp, modes, groups), ou...]
    reduce_sum x5 -> x0, other arithmetic: 39.3 us -> none  [the longest x1 25.3 us: per_device(): jnp.sum(gated_grad[:, None, :, :] * out_weights[None, :, :, :], axis=2)]
    unnamed x1 -> x0, blocking collectives: 23.1 us -> none
    all_gather x2 -> x0, waiting for transfers between devices: 21 us -> none  [entering(): gathered = jax.tree.map(lambda a: lax.all_gather(a, axis), part)]
    add x19 -> x0, other arithmetic: 14.6 us -> none  [the longest x7 6.87 us: counted(): return (earlier[0] + latter[0], span_decay * earlier[1] + latter[1])]
    pad x8 -> x0, local copies, waits for them, and re-layouts: 12.5 us -> none  [the longest x4 8.42 us: per_device(): lax.associative_scan(paired, (block_power, start_adj), axis=0, reverse=True)]
    mul x11 -> x0, other arithmetic: 11.7 us -> none  [the longest x1 5.51 us: per_device(): in_table = weight_t[:, None, :] * rev_powers * step_t[:, None, :]]
  transfers between devices with their start and end apart: 3 -> 0, of which waited for: 2 -> 0; matrix products, arithmetic and copies ran while one was open for 18% -> 0% of each run, Pallas kernels for 0% -> 0%
where the time goes in v2:
time: 59.4 us; the launch traced here: 59.1 us
  Pallas kernels  52.6 us (89%)
  local copies, waits for them, and re-layouts  5.8 us (10%)
  between operations  0.65 us (1%)
    pallas_call x1, Pallas kernels, per_device(): pl.pallas_call(functools.partial(fused_kernel, n, ntp, modes, groups), ou...  52.6 us
    unnamed x13, local copies, waits for them, and re-layouts  5.8 us

profile of v2, /device:TPU:0, one launch (start us, length us, event | category | flops | bytes accessed | tf_op | source)
XLA Modules:
  0.0 59.1 jit_solution(5714279936498413249)
XLA Ops:
  0.6 52.6 %fused.1 = (bf16[128,2048]{1,0:T(8,128)(2,1)}, bf16[128,2048]{1,0:T(8,128)(2,1)}, bf16[128,2048]{1,0:T(8,128)(2,1)}, f32[16,2048]{1,0:T(8,128)}, f32[16,2048]{1,0:T(8,128)}) custom-call(bf16[128,2048]{1,0:T(8,128)(2,1)} %go_ref.1, bf16[128,2048]{1,0:T(8,128)(2,1)} %q_ref.1, bf16[128,2048]{1,0:T(8,128)(2,1)} %k_ref.1, bf16[128,2048]{1,0:T(8,128)(2,1)} %v_ref.1, ...), custom_call_target="tpu_custom_call" | custom-call | tf_op jit(solution)/shard_map/fused/pallas_call | solution.py:312
  53.3 0.0 copy-start.1
  53.3 1.9 %copy.16 = bf16[128,2048]{1,0:T(8,128)(2,1)} copy(bf16[128,2048]{1,0:T(8,128)(2,1)} %get-tuple-element.20) | data formatting | bytes 1048576
  55.2 0.0 copy-done.1
  55.2 0.0 copy-start
  55.2 0.8 %copy.17 = bf16[128,2048]{1,0:T(8,128)(2,1)} copy(bf16[128,2048]{1,0:T(8,128)(2,1)S(1)} %copy-done.1) | data formatting | bytes 1048576
  56.0 0.4 copy-done
  56.5 0.0 copy-start.3
  56.5 0.8 %copy.18 = bf16[128,2048]{1,0:T(8,128)(2,1)} copy(bf16[128,2048]{1,0:T(8,128)(2,1)S(1)} %copy-done) | data formatting | bytes 1048576
  57.3 0.2 copy-done.3
  57.5 0.0 copy-start.2
  57.5 0.7 %copy.19 = f32[2048,16]{0,1:T(8,128)} copy(f32[2048,16]{0,1:T(8,128)S(1)} %bitcast.7) | data formatting | bytes 262144
  58.1 0.3 copy-done.2
  58.4 0.7 %copy.20 = f32[2048,16]{0,1:T(8,128)} copy(f32[2048,16]{0,1:T(8,128)S(1)} %bitcast.6) | data formatting | bytes 262144
Async XLA Ops:
  53.3 2.0 %copy-start.1 = (bf16[128,2048]{1,0:T(8,128)(2,1)S(1)}, bf16[128,2048]{1,0:T(8,128)(2,1)}, u32[]{:S(2)}) copy-start(bf16[128,2048]{1,0:T(8,128)(2,1)} %get-tuple-element.21) | copy-start | bytes 1572868
  55.2 1.2 %copy-start = (bf16[128,2048]{1,0:T(8,128)(2,1)S(1)}, bf16[128,2048]{1,0:T(8,128)(2,1)}, u32[]{:S(2)}) copy-start(bf16[128,2048]{1,0:T(8,128)(2,1)} %get-tuple-element.22) | copy-start | bytes 1572868
  56.5 1.0 %copy-start.3 = (f32[16,2048]{1,0:T(8,128)S(1)}, f32[16,2048]{1,0:T(8,128)}, u32[]{:S(2)}) copy-start(f32[16,2048]{1,0:T(8,128)} %get-tuple-element.13) | copy-start | bytes 393220
  57.5 1.0 %copy-start.2 = (f32[16,2048]{1,0:T(8,128)S(1)}, f32[16,2048]{1,0:T(8,128)}, u32[]{:S(2)}) copy-start(f32[16,2048]{1,0:T(8,128)} %get-tuple-element.14) | copy-start | bytes 393220

commit v3 on v2

--- a/solution.py
+++ b/solution.py
@@ -23,12 +23,15 @@
 def fused_kernel(
     n, ntp, modes, groups,
     go_ref, q_ref, k_ref, v_ref, lr_ref, res_ref,
-    gq_ref, gk_ref, gv_ref, dres_ref, drate_ref,
+    for_ref, back_ref, dres_ref, drate_ref, scale_ref,
     p_s, g_s, f_s, b_s, s_s, fr_s, br_s, sp_s, an_s,
-    ea_s, held, ca_s, raw_s, parts, red, gath, squares,
-    ex_send, ex_recv, rs_send, rs_recv, ag_send, ag_recv, sq_send, sq_recv,
+    ea_s, mate, pt_s, held, ca_s, raw_s, parts, red, gath, squares,
+    pa_send, pa_recv, ex_send, ex_recv, rs_send, rs_recv, ag_send, ag_recv, sq_send, sq_recv,
 ):
     me = lax.axis_index("ctx")
+    pair = me // 2
+    odd = lax.rem(me, 2)
+    pairs = n // 2
     total = n * ntp
     here = me * ntp + lax.axis_index("tp")
     rows, chans = go_ref.shape
@@ -99,14 +102,25 @@
 
         lax.fori_loop(0, per_group, chunk, 0)
 
+    def couple(g):
+        return pltpu.make_async_remote_copy(
+            src_ref=ea_s.at[g],
+            dst_ref=mate.at[g],
+            send_sem=pa_send.at[g],
+            recv_sem=pa_recv.at[g],
+            device_id={"ctx": pair * 2 + 1 - odd},
+            device_id_type=MESH,
+        )
+
     def exchange(g, k):
-        which = jnp.where(lax.rem(me + k, n) < me, 1, 0)
-        return pltpu.make_async_remote_copy(
-            src_ref=ea_s.at[g, which],
+        there = lax.rem(pair + k, pairs)
+        which = jnp.where(there < pair, 1, 0)
+        return pltpu.make_async_remote_copy(
+            src_ref=pt_s.at[g, which],
             dst_ref=held.at[g, k - 1],
             send_sem=ex_send.at[g, k - 1],
             recv_sem=ex_recv.at[g, k - 1],
-            device_id=peer(k),
+            device_id={"ctx": there * 2 + odd},
             device_id_type=MESH,
         )
 
@@ -141,17 +155,33 @@
             device_id_type=MESH,
         )
 
+    def rates(g):
+        at = pl.ds(pl.multiple_of(g * per_group * LANES, LANES), per_group * LANES)
+        return jnp.exp(lr_ref[:, at])
+
+    def join(g):
+        couple(g).wait_recv()
+        across = jnp.exp(-rates(g) * rows)
+        mine, other = ea_s[g], mate[g]
+        early = jnp.where(odd == 1, other, mine)
+        late = jnp.where(odd == 1, mine, other)
+        pt_s[g, 0] = across * early[0] + late[0]
+        pt_s[g, 1] = early[1] + across * late[1]
+        for k in range(1, pairs):
+            exchange(g, k).start()
+
     def carry(g):
-        at = pl.ds(pl.multiple_of(g * per_group * LANES, LANES), per_group * LANES)
-        rate = jnp.exp(lr_ref[:, at])
+        rate = rates(g)
         ca_s[...] = jnp.zeros_like(ca_s)
-        for k in range(1, n):
+        for k in range(1, pairs):
             exchange(g, k).wait_recv()
-            origin = lax.rem(me - k + n, n)
-            which = jnp.where(origin < me, 0, 1)
-            gap = jnp.where(origin < me, me - origin, origin - me) - 1
-            power = jnp.exp(-rate * (gap * rows).astype(jnp.float32))
+            origin = lax.rem(pair - k + pairs, pairs)
+            which = jnp.where(origin < pair, 0, 1)
+            gap = jnp.where(origin < pair, pair - origin, origin - pair) - 1
+            power = jnp.exp(-rate * (gap * (2 * rows)).astype(jnp.float32))
             ca_s[which] += power * held[g, k - 1]
+        near = 1 - odd
+        ca_s[near] = mate[g, near] + jnp.exp(-rate * rows) * ca_s[near]
 
     def main(g):
         def chunk(c, _):
@@ -207,10 +237,8 @@
                         br_s[pl.ds(i, SUB, stride=span), :] = b_s[i] + b
                 raw += [jnp.sum(r, axis=0, keepdims=True) for r in rw]
                 lag += [jnp.sum(l, axis=0, keepdims=True) for l in lg]
-            gq_ref[:, at] = (go_ref[:, at].astype(jnp.float32) * fr_s[...]).astype(jnp.bfloat16)
-            back = br_s[...]
-            gk_ref[:, at] = (back * v_ref[:, at].astype(jnp.float32)).astype(jnp.bfloat16)
-            gv_ref[:, at] = (back * k_ref[:, at].astype(jnp.float32)).astype(jnp.bfloat16)
+            for_ref[:, at] = fr_s[...]
+            back_ref[:, at] = br_s[...]
             raw_weight = jnp.concatenate(raw, axis=0)
             lag_total = decay * jnp.concatenate(lag, axis=0)
             both = (root * raw_weight, weight * (0.5 * raw_weight - rate * lag_total))
@@ -226,8 +254,8 @@
 
     def first_stage(g, _):
         ends(g)
-        for k in range(1, n):
-            exchange(g, k).start()
+        couple(g).start()
+        join(g - 1)
         return 0
 
     def second_stage(g, _):
@@ -239,9 +267,9 @@
 
     ends(0)
     pl.semaphore_wait(barrier, total - 1)
-    for k in range(1, n):
-        exchange(0, k).start()
+    couple(0).start()
     lax.fori_loop(1, groups, first_stage, 0)
+    join(groups - 1)
     lax.fori_loop(0, groups, second_stage, 0)
 
     sums = zero
@@ -258,9 +286,9 @@
         norm(q).start()
         return 0
 
-    lax.fori_loop(1, total, norm_start, 0)
     for k in range(1, n):
         gather(k).start()
+    lax.fori_loop(1, total, norm_start, 0)
     gath[me] = red[...]
 
     def norm_wait(q, _):
@@ -270,6 +298,7 @@
     lax.fori_loop(1, total, norm_wait, 0)
     square = jnp.sum(jnp.sum(squares[...], axis=0), keepdims=True)
     scale = jnp.minimum(1.0, CLIP_NORM / jnp.sqrt(square + 1e-06))
+    scale_ref[...] = jnp.broadcast_to(scale, (SUB, LANES))
     for k in range(1, n):
         gather(k).wait_recv()
     for g in range(groups):
@@ -279,11 +308,13 @@
                 tile = c * pieces + piece
                 low = piece % (pieces // 2) * SUB
                 ref = dres_ref if piece < pieces // 2 else drate_ref
-                ref[low : low + SUB, at] = gath[tile // own, g, tile % own] * scale
+                ref[low : low + SUB, at] = gath[tile // own, g, tile % own]
 
     def drain(g, _):
+        couple(g).wait_send()
+        for k in range(1, pairs):
+            exchange(g, k).wait_send()
         for k in range(1, n):
-            exchange(g, k).wait_send()
             scatter(g, k).wait_send()
         return 0
 
@@ -307,11 +338,11 @@
     tile = lambda *lead: pltpu.VMEM((*lead, SUB, LANES), f32)
     flags = lambda *dims: pltpu.SemaphoreType.DMA(dims)
     flat = buffer(rows, LANES)
-    wide_out = shape((rows, chans), jnp.bfloat16)
+    wide_out = shape((rows, chans), f32)
     tall_out = shape((modes, chans), f32)
-    grad_query, grad_key, grad_value, d_res, d_rate = pl.pallas_call(
+    filtered, back_filtered, d_res, d_rate, scale = pl.pallas_call(
         functools.partial(fused_kernel, n, ntp, modes, groups),
-        out_shape=(wide_out,) * 3 + (tall_out,) * 2,
+        out_shape=(wide_out,) * 2 + (tall_out,) * 2 + (shape((SUB, LANES), f32),),
         in_specs=[vmem] * 6,
         out_specs=(vmem,) * 5,
         scratch_shapes=[
@@ -319,14 +350,17 @@
             buffer(modes, SUB, chans),
             buffer(modes, SUB, chans),
             buffer(groups, 2, modes, width),
-            buffer(groups, n - 1, modes, width),
+            buffer(groups, 2, modes, width),
+            buffer(groups, 2, modes, width),
+            buffer(groups, n // 2 - 1, modes, width),
             buffer(2, modes, width),
             tile(groups, own * n),
             tile(groups, n - 1, own),
             tile(groups, own),
             tile(n, groups, own),
             tile(n * ntp),
-            flags(groups, n - 1), flags(groups, n - 1),
+            flags(groups), flags(groups),
+            flags(groups, n // 2 - 1), flags(groups, n // 2 - 1),
             flags(groups, n - 1), flags(groups, n - 1),
             flags(n - 1), flags(n - 1),
             flags(n * ntp - 1), flags(n * ntp - 1),
@@ -336,7 +370,11 @@
         ),
         name="fused",
     )(grad_out, query_in, key_in, value_in, log_rate.T, residue.T)
-    return grad_query, grad_key, grad_value, d_res.T, d_rate.T
+    grad_query = (grad_out.astype(f32) * filtered).astype(jnp.bfloat16)
+    grad_key = (back_filtered * value_in.astype(f32)).astype(jnp.bfloat16)
+    grad_value = (back_filtered * key_in.astype(f32)).astype(jnp.bfloat16)
+    factor = scale[0, 0]
+    return grad_query, grad_key, grad_value, d_res.T * factor, d_rate.T * factor
 
 
 def solution(mesh):

time: 59.4 us -> 52.7 us (0.89)
  Pallas kernels: 52.6 us -> 45.4 us
  other arithmetic: 0 us -> 5.24 us
  local copies, waits for them, and re-layouts: 5.8 us -> 1.26 us
    pallas_call x1, Pallas kernels: 52.6 us -> 45.4 us  [per_device(): pl.pallas_call(functools.partial(fused_kernel, n, ntp, modes, groups), ou...]
    unnamed x13 -> x6, local copies, waits for them, and re-layouts: 5.8 us -> 0.01 us
    convert_element_type x0 -> x1, other arithmetic: none -> 2.91 us  [per_device(): grad_value = (back_filtered * key_in.astype(f32)).astype(jnp.bfloat16)]
    mul x0 -> x1, other arithmetic: none -> 2.33 us  [per_device(): d_rate.T * factor]
    slice x0 -> x1, local copies, waits for them, and re-layouts: none -> 1.24 us  [per_device(): factor = scale[0, 0]]
where the time goes in v3:
time: 52.7 us; the launch traced here: 52.5 us
  Pallas kernels  45.4 us (86%)
  other arithmetic  5.24 us (10%)
  local copies, waits for them, and re-layouts  1.26 us (2%)
  between operations  0.67 us (1%)
    pallas_call x1, Pallas kernels, per_device(): pl.pallas_call(functools.partial(fused_kernel, n, ntp, modes, groups), ou...  45.4 us
    convert_element_type x1, other arithmetic, per_device(): grad_value = (back_filtered * key_in.astype(f32)).astype(jnp.bfloat16)  2.91 us
    mul x1, other arithmetic, per_device(): d_rate.T * factor  2.33 us
    slice x1, local copies, waits for them, and re-layouts, per_device(): factor = scale[0, 0]  1.24 us

profile of v3, /device:TPU:0, one launch (start us, length us, event | category | flops | bytes accessed | tf_op | source)
XLA Modules:
  0.0 52.5 jit_solution(10479028871555959129)
XLA Ops:
  0.6 0.0 copy-start.1
  0.6 0.0 copy-start.2
  0.7 45.4 %fused.1 = (f32[128,2048]{1,0:T(8,128)}, f32[128,2048]{1,0:T(8,128)}, f32[16,2048]{1,0:T(8,128)}, f32[16,2048]{1,0:T(8,128)}, f32[8,128]{1,0:T(8,128)}) custom-call(bf16[128,2048]{1,0:T(8,128)(2,1)} %go_ref.1, bf16[128,2048]{1,0:T(8,128)(2,1)} %q_ref.1, bf16[128,2048]{1,0:T(8,128)(2,1)} %k_ref.1, bf16[128,2048]{1,0:T(8,128)(2,1)} %v_ref.1, ...), custom_call_target="tpu_custom_call" | custom-call | tf_op jit(solution)/shard_map/fused/pallas_call | solution.py:343
  46.0 0.0 copy-start
  46.0 1.2 %slice.3 = f32[1,1]{1,0:T(1,128)} slice(f32[8,128]{1,0:T(8,128)} %get-tuple-element.13), slice={[0:1], [0:1]} | slice | bytes 8 | tf_op jit(solution)/shard_map/slice | solution.py:376
  47.3 2.3 %multiply_bitcast_fusion = (f32[2048,16]{0,1:T(8,128)}, f32[2048,16]{0,1:T(8,128)}) fusion(f32[16,2048]{1,0:T(8,128)} %get-tuple-element.14, f32[]{:T(128)} %bitcast.2, f32[16,2048]{1,0:T(8,128)} %get-tuple-element.12), kind=kLoop, calls=%fused_computation.3 | loop fusion | flops 65536 | bytes 524292 | tf_op jit(solution)/shard_map/mul | solution.py:377
  49.6 0.0 copy-done.1
  49.6 0.0 copy-done.2
  49.6 0.0 copy-done
  49.6 2.9 %multiply_convert_fusion = (bf16[128,2048]{1,0:T(8,128)(2,1)}, bf16[128,2048]{1,0:T(8,128)(2,1)}, bf16[128,2048]{1,0:T(8,128)(2,1)}) fusion(f32[128,2048]{1,0:T(8,128)} %get-tuple-element.11, bf16[128,2048]{1,0:T(8,128)(2,1)S(1)} %copy-done.1, bf16[128,2048]{1,0:T(8,128)(2,1)S(1)} %copy-done.2, f32[128,2048]{1,0:T(8,128)} %get-tuple-element.10, ...), kind=kLoop, calls=%fused_computation | loop fusion | flops 2359296 | bytes 5242880 | tf_op jit(solution)/shard_map/convert_element_type | solution.py:375
Async XLA Ops:
  0.6 49.0 %copy-start.1 = (bf16[128,2048]{1,0:T(8,128)(2,1)S(1)}, bf16[128,2048]{1,0:T(8,128)(2,1)}, u32[]{:S(2)}) copy-start(bf16[128,2048]{1,0:T(8,128)(2,1)} %k_ref.1) | copy-start | bytes 1572868
  0.6 49.0 %copy-start.2 = (bf16[128,2048]{1,0:T(8,128)(2,1)S(1)}, bf16[128,2048]{1,0:T(8,128)(2,1)}, u32[]{:S(2)}) copy-start(bf16[128,2048]{1,0:T(8,128)(2,1)} %v_ref.1) | copy-start | bytes 1572868
  46.0 3.6 %copy-start = (bf16[128,2048]{1,0:T(8,128)(2,1)S(1)}, bf16[128,2048]{1,0:T(8,128)(2,1)}, u32[]{:S(2)}) copy-start(bf16[128,2048]{1,0:T(8,128)(2,1)} %go_ref.1) | copy-start | bytes 1572868

commit v4 on v3

--- a/solution.py
+++ b/solution.py
@@ -20,12 +20,18 @@
     return jnp.where(keep, moved, 0.0)
 
 
+def total_of(terms):
+    while len(terms) > 1:
+        terms = [x + y for x, y in zip(terms[::2], terms[1::2])]
+    return terms[0]
+
+
 def fused_kernel(
     n, ntp, modes, groups,
     go_ref, q_ref, k_ref, v_ref, lr_ref, res_ref,
-    for_ref, back_ref, dres_ref, drate_ref, scale_ref,
+    for_ref, back_ref, dres_ref, drate_ref,
     p_s, g_s, f_s, b_s, s_s, fr_s, br_s, sp_s, an_s,
-    ea_s, mate, pt_s, held, ca_s, raw_s, parts, red, gath, squares,
+    ea_s, mate, pt_s, held, ca_s, raw_s, parts, red, gath, sums, squares,
     pa_send, pa_recv, ex_send, ex_recv, rs_send, rs_recv, ag_send, ag_recv, sq_send, sq_recv,
 ):
     me = lax.axis_index("ctx")
@@ -42,7 +48,7 @@
     row = lax.broadcasted_iota(jnp.int32, (SUB, LANES), 0)
     level = row.astype(jnp.float32)
     zero = jnp.zeros((SUB, LANES), jnp.float32)
-    size = 4
+    size = 8
 
     def place(q):
         other = lax.rem(here + q, total)
@@ -81,13 +87,12 @@
                 group = range(first, min(modes, first + 8))
                 a = [wide(decay, m) for m in group]
                 s = [zero] * len(a)
+                t = [zero] * len(a)
                 for i in range(span):
                     x = p_s[pl.ds(i, SUB, stride=span), :]
+                    y = g_s[pl.ds(span - 1 - i, SUB, stride=span), :]
                     s = [aa * ss + x for aa, ss in zip(a, s)]
-                t = [zero] * len(a)
-                for i in reversed(range(span)):
-                    x = g_s[pl.ds(i, SUB, stride=span), :]
-                    t = [aa * tt + x for aa, tt in zip(a, t)]
+                    t = [aa * tt + y for aa, tt in zip(a, t)]
                 for slot, m in enumerate(group):
                     x, y = s[slot], t[slot]
                     for far, table in zip((1, 2, 4), steps):
@@ -135,12 +140,12 @@
             device_id_type=MESH,
         )
 
-    def gather(k):
+    def gather(g, k):
         return pltpu.make_async_remote_copy(
-            src_ref=red,
-            dst_ref=gath.at[me],
-            send_sem=ag_send.at[k - 1],
-            recv_sem=ag_recv.at[k - 1],
+            src_ref=red.at[g],
+            dst_ref=gath.at[g, me],
+            send_sem=ag_send.at[g, k - 1],
+            recv_sem=ag_recv.at[g, k - 1],
             device_id=peer(k),
             device_id_type=MESH,
         )
@@ -217,7 +222,7 @@
                     for j in range(size):
                         s_s[i * size + j] = s[j]
                     rw = [r + y * ss for r, ss in zip(rw, s)]
-                    f = (w[0] * s[0] + w[1] * s[1]) + (w[2] * s[2] + w[3] * s[3])
+                    f = total_of([ww * ss for ww, ss in zip(w, s)])
                     if first == 0:
                         f_s[i] = f
                     elif first + size < modes:
@@ -228,7 +233,7 @@
                     y = g_s[pl.ds(i, SUB, stride=span), :]
                     lg = [l + s_s[i * size + j] * t[j] for j, l in enumerate(lg)]
                     t = [aa * tt + y for aa, tt in zip(a, t)]
-                    b = (w[0] * t[0] + w[1] * t[1]) + (w[2] * t[2] + w[3] * t[3])
+                    b = total_of([ww * tt for ww, tt in zip(w, t)])
                     if first == 0:
                         b_s[i] = b
                     elif first + size < modes:
@@ -258,38 +263,47 @@
         join(g - 1)
         return 0
 
-    def second_stage(g, _):
+    def produce(g):
         carry(g)
         main(g)
         for k in range(1, n):
             scatter(g, k).start()
-        return 0
-
-    ends(0)
-    pl.semaphore_wait(barrier, total - 1)
-    couple(0).start()
-    lax.fori_loop(1, groups, first_stage, 0)
-    join(groups - 1)
-    lax.fori_loop(0, groups, second_stage, 0)
-
-    sums = zero
-    for g in range(groups):
+
+    def finish(g):
         mine = raw_s[g, pl.ds(me * own, own)]
         for k in range(1, n):
             scatter(g, k).wait_recv()
             mine = mine + parts[g, k - 1]
         red[g] = mine
-        sums = sums + jnp.sum(mine * mine, axis=0)
-    squares[here] = sums
+        for k in range(1, n):
+            gather(g, k).start()
+        gath[g, me] = mine
+        sums[...] += jnp.sum(mine * mine, axis=0)
+
+    def second_stage(g, _):
+        produce(g)
+        finish(g - 1)
+        return 0
+
+    sums[...] = zero
+    ends(0)
+    pl.semaphore_wait(barrier, total - 1)
+    couple(0).start()
+    lax.fori_loop(1, groups, first_stage, 0)
+    if groups == 1:
+        join(0)
+    produce(0)
+    if groups > 1:
+        join(groups - 1)
+    lax.fori_loop(1, groups, second_stage, 0)
+    finish(groups - 1)
+    squares[here] = sums[...]
 
     def norm_start(q, _):
         norm(q).start()
         return 0
 
-    for k in range(1, n):
-        gather(k).start()
     lax.fori_loop(1, total, norm_start, 0)
-    gath[me] = red[...]
 
     def norm_wait(q, _):
         norm(q).wait()
@@ -298,17 +312,16 @@
     lax.fori_loop(1, total, norm_wait, 0)
     square = jnp.sum(jnp.sum(squares[...], axis=0), keepdims=True)
     scale = jnp.minimum(1.0, CLIP_NORM / jnp.sqrt(square + 1e-06))
-    scale_ref[...] = jnp.broadcast_to(scale, (SUB, LANES))
-    for k in range(1, n):
-        gather(k).wait_recv()
     for g in range(groups):
+        for k in range(1, n):
+            gather(g, k).wait_recv()
         for c in range(per_group):
             at = pl.ds((g * per_group + c) * LANES, LANES)
             for piece in range(pieces):
                 tile = c * pieces + piece
                 low = piece % (pieces // 2) * SUB
                 ref = dres_ref if piece < pieces // 2 else drate_ref
-                ref[low : low + SUB, at] = gath[tile // own, g, tile % own]
+                ref[low : low + SUB, at] = gath[g, tile // own, tile % own] * scale
 
     def drain(g, _):
         couple(g).wait_send()
@@ -316,12 +329,10 @@
             exchange(g, k).wait_send()
         for k in range(1, n):
             scatter(g, k).wait_send()
+            gather(g, k).wait_send()
         return 0
 
     lax.fori_loop(0, groups, drain, 0)
-    for k in range(1, n):
-        gather(k).wait_send()
-
 
 def per_device(n, ntp, grad_out, query_in, key_in, value_in, residue, log_rate):
     rows, chans = grad_out.shape
@@ -340,13 +351,13 @@
     flat = buffer(rows, LANES)
     wide_out = shape((rows, chans), f32)
     tall_out = shape((modes, chans), f32)
-    filtered, back_filtered, d_res, d_rate, scale = pl.pallas_call(
+    filtered, back_filtered, d_res, d_rate = pl.pallas_call(
         functools.partial(fused_kernel, n, ntp, modes, groups),
-        out_shape=(wide_out,) * 2 + (tall_out,) * 2 + (shape((SUB, LANES), f32),),
+        out_shape=(wide_out,) * 2 + (tall_out,) * 2,
         in_specs=[vmem] * 6,
-        out_specs=(vmem,) * 5,
+        out_specs=(vmem,) * 4,
         scratch_shapes=[
-            flat, flat, tile(span), tile(span), tile(4 * span), flat, flat,
+            flat, flat, tile(span), tile(span), tile(8 * span), flat, flat,
             buffer(modes, SUB, chans),
             buffer(modes, SUB, chans),
             buffer(groups, 2, modes, width),
@@ -357,12 +368,13 @@
             tile(groups, own * n),
             tile(groups, n - 1, own),
             tile(groups, own),
-            tile(n, groups, own),
+            tile(groups, n, own),
+            tile(),
             tile(n * ntp),
             flags(groups), flags(groups),
             flags(groups, n // 2 - 1), flags(groups, n // 2 - 1),
             flags(groups, n - 1), flags(groups, n - 1),
-            flags(n - 1), flags(n - 1),
+            flags(groups, n - 1), flags(groups, n - 1),
             flags(n * ntp - 1), flags(n * ntp - 1),
         ],
         compiler_params=pltpu.CompilerParams(
@@ -373,8 +385,7 @@
     grad_query = (grad_out.astype(f32) * filtered).astype(jnp.bfloat16)
     grad_key = (back_filtered * value_in.astype(f32)).astype(jnp.bfloat16)
     grad_value = (back_filtered * key_in.astype(f32)).astype(jnp.bfloat16)
-    factor = scale[0, 0]
-    return grad_query, grad_key, grad_value, d_res.T * factor, d_rate.T * factor
+    return grad_query, grad_key, grad_value, d_res.T, d_rate.T
 
 
 def solution(mesh):

time: 52.7 us -> 50.3 us (0.954)
  other arithmetic: 5.24 us -> 2.93 us
    mul x1 -> x0, other arithmetic: 2.33 us -> none  [per_device(): d_rate.T * factor]
    unnamed x6 -> x12, local copies, waits for them, and re-layouts: 0.01 us -> 1.62 us
    slice x1 -> x0, local copies, waits for them, and re-layouts: 1.24 us -> none  [per_device(): factor = scale[0, 0]]
where the time goes in v4:
time: 50.3 us; the launch traced here: 50.2 us
  Pallas kernels  44.9 us (89%)
  other arithmetic  2.93 us (6%)
  local copies, waits for them, and re-layouts  1.62 us (3%)
  between operations  0.7 us (1%)
    pallas_call x1, Pallas kernels, per_device(): pl.pallas_call(functools.partial(fused_kernel, n, ntp, modes, groups), ou...  44.9 us
    convert_element_type x1, other arithmetic, per_device(): grad_value = (back_filtered * key_in.astype(f32)).astype(jnp.bfloat16)  2.93 us
    unnamed x12, local copies, waits for them, and re-layouts  1.62 us

profile of v4, /device:TPU:0, one launch (start us, length us, event | category | flops | bytes accessed | tf_op | source)
XLA Modules:
  0.0 50.2 jit_solution(14797879254444931419)
XLA Ops:
  0.6 0.0 copy-start
  0.6 0.0 copy-start.1
  0.7 0.0 copy-start.2
  0.7 44.9 %fused.1 = (f32[128,2048]{1,0:T(8,128)}, f32[128,2048]{1,0:T(8,128)}, f32[16,2048]{1,0:T(8,128)}, f32[16,2048]{1,0:T(8,128)}) custom-call(bf16[128,2048]{1,0:T(8,128)(2,1)} %go_ref.1, bf16[128,2048]{1,0:T(8,128)(2,1)} %q_ref.1, bf16[128,2048]{1,0:T(8,128)(2,1)} %k_ref.1, bf16[128,2048]{1,0:T(8,128)(2,1)} %v_ref.1, f32[16,2048]{1,0:T(8,128)} %bitcast.4, ...), custom_call_target="tpu_custom_call" | custom-call | tf_op jit(solution)/shard_map/fused/pallas_call | solution.py:354
  45.6 0.0 copy-done
  45.6 0.0 copy-done.1
  45.6 0.0 copy-done.2
  45.6 0.0 copy-start.4
  45.6 2.9 %multiply_convert_fusion = (bf16[128,2048]{1,0:T(8,128)(2,1)}, bf16[128,2048]{1,0:T(8,128)(2,1)}, bf16[128,2048]{1,0:T(8,128)(2,1)}) fusion(f32[128,2048]{1,0:T(8,128)} %get-tuple-element.10, bf16[128,2048]{1,0:T(8,128)(2,1)S(1)} %copy-done.1, bf16[128,2048]{1,0:T(8,128)(2,1)S(1)} %copy-done.2, f32[128,2048]{1,0:T(8,128)} %get-tuple-element.9, ...), kind=kLoop, calls=%fused_computation | loop fusion | flops 2359296 | bytes 5242880 | tf_op jit(solution)/shard_map/convert_element_type | solution.py:387
  48.5 0.0 copy-done.4
  48.6 0.0 copy-start.3
  48.6 0.7 %copy.13 = f32[2048,16]{0,1:T(8,128)} copy(f32[2048,16]{0,1:T(8,128)S(1)} %bitcast.7) | data formatting | bytes 262144
  49.2 0.3 copy-done.3
  49.5 0.7 %copy.14 = f32[2048,16]{0,1:T(8,128)} copy(f32[2048,16]{0,1:T(8,128)S(1)} %bitcast.6) | data formatting | bytes 262144
Async XLA Ops:
  0.6 44.9 %copy-start = (bf16[128,2048]{1,0:T(8,128)(2,1)S(1)}, bf16[128,2048]{1,0:T(8,128)(2,1)}, u32[]{:S(2)}) copy-start(bf16[128,2048]{1,0:T(8,128)(2,1)} %go_ref.1) | copy-start | bytes 1572868
  0.6 44.9 %copy-start.1 = (bf16[128,2048]{1,0:T(8,128)(2,1)S(1)}, bf16[128,2048]{1,0:T(8,128)(2,1)}, u32[]{:S(2)}) copy-start(bf16[128,2048]{1,0:T(8,128)(2,1)} %k_ref.1) | copy-start | bytes 1572868
  0.7 44.9 %copy-start.2 = (bf16[128,2048]{1,0:T(8,128)(2,1)S(1)}, bf16[128,2048]{1,0:T(8,128)(2,1)}, u32[]{:S(2)}) copy-start(bf16[128,2048]{1,0:T(8,128)(2,1)} %v_ref.1) | copy-start | bytes 1572868
  45.6 2.9 %copy-start.4 = (f32[16,2048]{1,0:T(8,128)S(1)}, f32[16,2048]{1,0:T(8,128)}, u32[]{:S(2)}) copy-start(f32[16,2048]{1,0:T(8,128)} %get-tuple-element.11) | copy-start | bytes 393220
  48.6 1.0 %copy-start.3 = (f32[16,2048]{1,0:T(8,128)S(1)}, f32[16,2048]{1,0:T(8,128)}, u32[]{:S(2)}) copy-start(f32[16,2048]{1,0:T(8,128)} %get-tuple-element.12) | copy-start | bytes 393220

commit v5 on v4

--- a/solution.py
+++ b/solution.py
@@ -264,7 +264,6 @@
         return 0
 
     def produce(g):
-        carry(g)
         main(g)
         for k in range(1, n):
             scatter(g, k).start()
@@ -281,6 +280,7 @@
         sums[...] += jnp.sum(mine * mine, axis=0)
 
     def second_stage(g, _):
+        carry(g)
         produce(g)
         finish(g - 1)
         return 0
@@ -292,9 +292,10 @@
     lax.fori_loop(1, groups, first_stage, 0)
     if groups == 1:
         join(0)
-    produce(0)
+    carry(0)
     if groups > 1:
         join(groups - 1)
+    produce(0)
     lax.fori_loop(1, groups, second_stage, 0)
     finish(groups - 1)
     squares[here] = sums[...]

time: 50.3 us -> 50.9 us (1.012)
  Pallas kernels: 44.9 us -> 45.5 us
    pallas_call x1, Pallas kernels: 44.9 us -> 45.5 us  [per_device(): pl.pallas_call(functools.partial(fused_kernel, n, ntp, modes, groups), ou...]
where the time goes in v5:
time: 50.9 us; the launch traced here: 50.7 us
  Pallas kernels  45.5 us (89%)
  other arithmetic  2.93 us (6%)
  local copies, waits for them, and re-layouts  1.62 us (3%)
  between operations  0.7 us (1%)
    pallas_call x1, Pallas kernels, per_device(): pl.pallas_call(functools.partial(fused_kernel, n, ntp, modes, groups), ou...  45.5 us
    convert_element_type x1, other arithmetic, per_device(): grad_value = (back_filtered * key_in.astype(f32)).astype(jnp.bfloat16)  2.93 us
    unnamed x12, local copies, waits for them, and re-layouts  1.62 us

profile of v5, /device:TPU:0, one launch (start us, length us, event | category | flops | bytes accessed | tf_op | source)
XLA Modules:
  0.0 50.7 jit_solution(11303462971758672262)
XLA Ops:
  0.6 0.0 copy-start
  0.6 0.0 copy-start.1
  0.7 0.0 copy-start.2
  0.7 45.5 %fused.1 = (f32[128,2048]{1,0:T(8,128)}, f32[128,2048]{1,0:T(8,128)}, f32[16,2048]{1,0:T(8,128)}, f32[16,2048]{1,0:T(8,128)}) custom-call(bf16[128,2048]{1,0:T(8,128)(2,1)} %go_ref.1, bf16[128,2048]{1,0:T(8,128)(2,1)} %q_ref.1, bf16[128,2048]{1,0:T(8,128)(2,1)} %k_ref.1, bf16[128,2048]{1,0:T(8,128)(2,1)} %v_ref.1, f32[16,2048]{1,0:T(8,128)} %bitcast.4, ...), custom_call_target="tpu_custom_call" | custom-call | tf_op jit(solution)/shard_map/fused/pallas_call | solution.py:355
  46.2 0.0 copy-done
  46.2 0.0 copy-done.1
  46.2 0.0 copy-done.2
  46.2 0.0 copy-start.4
  46.2 2.9 %multiply_convert_fusion = (bf16[128,2048]{1,0:T(8,128)(2,1)}, bf16[128,2048]{1,0:T(8,128)(2,1)}, bf16[128,2048]{1,0:T(8,128)(2,1)}) fusion(f32[128,2048]{1,0:T(8,128)} %get-tuple-element.10, bf16[128,2048]{1,0:T(8,128)(2,1)S(1)} %copy-done.1, bf16[128,2048]{1,0:T(8,128)(2,1)S(1)} %copy-done.2, f32[128,2048]{1,0:T(8,128)} %get-tuple-element.9, ...), kind=kLoop, calls=%fused_computation | loop fusion | flops 2359296 | bytes 5242880 | tf_op jit(solution)/shard_map/convert_element_type | solution.py:388
  49.1 0.0 copy-done.4
  49.1 0.0 copy-start.3
  49.1 0.7 %copy.13 = f32[2048,16]{0,1:T(8,128)} copy(f32[2048,16]{0,1:T(8,128)S(1)} %bitcast.7) | data formatting | bytes 262144
  49.8 0.3 copy-done.3
  50.1 0.7 %copy.14 = f32[2048,16]{0,1:T(8,128)} copy(f32[2048,16]{0,1:T(8,128)S(1)} %bitcast.6) | data formatting | bytes 262144
Async XLA Ops:
  0.6 45.5 %copy-start = (bf16[128,2048]{1,0:T(8,128)(2,1)S(1)}, bf16[128,2048]{1,0:T(8,128)(2,1)}, u32[]{:S(2)}) copy-start(bf16[128,2048]{1,0:T(8,128)(2,1)} %go_ref.1) | copy-start | bytes 1572868
  0.6 45.5 %copy-start.1 = (bf16[128,2048]{1,0:T(8,128)(2,1)S(1)}, bf16[128,2048]{1,0:T(8,128)(2,1)}, u32[]{:S(2)}) copy-start(bf16[128,2048]{1,0:T(8,128)(2,1)} %k_ref.1) | copy-start | bytes 1572868
  0.7 45.5 %copy-start.2 = (bf16[128,2048]{1,0:T(8,128)(2,1)S(1)}, bf16[128,2048]{1,0:T(8,128)(2,1)}, u32[]{:S(2)}) copy-start(bf16[128,2048]{1,0:T(8,128)(2,1)} %v_ref.1) | copy-start | bytes 1572868
  46.2 2.9 %copy-start.4 = (f32[16,2048]{1,0:T(8,128)S(1)}, f32[16,2048]{1,0:T(8,128)}, u32[]{:S(2)}) copy-start(f32[16,2048]{1,0:T(8,128)} %get-tuple-element.11) | copy-start | bytes 393220
  49.1 1.0 %copy-start.3 = (f32[16,2048]{1,0:T(8,128)S(1)}, f32[16,2048]{1,0:T(8,128)}, u32[]{:S(2)}) copy-start(f32[16,2048]{1,0:T(8,128)} %get-tuple-element.12) | copy-start | bytes 393220
